TPU v7x, 512 devices: a whole 4x8x8 slice. The times are simulated.
512 devices in a mesh: gz: 128 (over z, y, core), gy: 4 (over x).
Axes of the slice: x: 4, y: 8, z: 8, core: 2. Of those that a mesh axis runs over, the one named last changes fastest.
Arguments:
- level_input: bfloat16 [128, 32, 64, 128], P('gz', 'gy'), may hold values from -6 to 6
- pre_activation: bfloat16 [128, 32, 64, 128], P('gz', 'gy'), may hold values from -6 to 6
- conv_weight: bfloat16 [3, 3, 3, 128, 128], replicated, may hold values from -0.109375 to 0.109375
- down_weight: bfloat16 [2, 2, 2, 128, 256], replicated, may hold values from -0.1875 to 0.1875
- skip_cotangent: bfloat16 [128, 32, 64, 128], P('gz', 'gy'), may hold values from -12 to 12
- deep_cotangent: bfloat16 [64, 16, 32, 256], P(None, 'gy', None, 'gz'), may hold values from -12 to 12
Outputs:
- input_grad: bfloat16 [128, 32, 64, 128], P('gz', 'gy')
- conv_weight_grad: bfloat16 [3, 3, 3, 128, 128], replicated
- down_weight_grad: bfloat16 [2, 2, 2, 128, 256], replicated
All inputs are finite; a program needn't handle non-finite values.
Results may differ from a plain program's by a relative error of at most 0.0054.
Values may be sent and summed in bfloat16 or wider, within the bound.
A program may use at most 64 MiB of HBM per device.

v0:
```python
import math

import jax
import jax.numpy as jnp
from jax import lax
from jax.sharding import PartitionSpec as P


def swapped(array, axis, bit):
    return lax.ppermute(array, axis, [(i, i ^ 1 << bit) for i in range(lax.axis_size(axis))])


def extended(cells, sides, width):
    for axis, dim in sides:
        count = lax.axis_size(axis)
        ends = count - 1
        head = lax.slice_in_dim(cells, 0, width, axis=dim)
        tail = lax.slice_in_dim(cells, cells.shape[dim] - width, cells.shape[dim], axis=dim)
        cells = jnp.concatenate(
            [
                lax.ppermute(tail, axis, [(i, (i + 1) % count) for i in range(ends)]),
                cells,
                lax.ppermute(head, axis, [((i + 1) % count, i) for i in range(ends)]),
            ],
            axis=dim,
        )
    return cells


def per_device(
    level_input, pre_activation, conv_weight, down_weight, skip_cotangent, deep_cotangent
):
    row_count = level_input.shape[1]
    col_count = level_input.shape[2]
    channels = level_input.shape[3]
    plane_count = deep_cotangent.shape[0]
    deep_rows = deep_cotangent.shape[1]
    deep_cols = deep_cotangent.shape[2]
    deep_share = deep_cotangent.shape[3]
    parity = lax.axis_index("gz") % 2
    halved = deep_cotangent.reshape(2 * plane_count, deep_rows // 2, deep_cols, deep_share)
    own_half = lax.all_to_all(halved, "gz", split_axis=0, concat_axis=3, tiled=True)[0]
    pair_half = swapped(own_half, "gz", 0)
    even_plane = parity == 0
    top_half = jnp.where(even_plane, own_half, pair_half)
    low_half = jnp.where(even_plane, pair_half, own_half)
    deep_grad = jnp.concatenate([top_half, low_half], axis=0)
    down_slice = lax.dynamic_index_in_dim(down_weight, parity, 0, keepdims=False)
    down_part = jnp.einsum(
        "yxo,bcio->ybxci", deep_grad, down_slice, preferred_element_type=jnp.float32
    )
    down_part = down_part.reshape(row_count, col_count, channels)
    hidden_grad = down_part + skip_cotangent[0].astype(jnp.float32)
    pre_plane = pre_activation[0]
    masked_grad = jnp.where(pre_plane > 0, hidden_grad, jnp.zeros_like(hidden_grad)).astype(
        jnp.bfloat16
    )
    hidden = jnp.maximum(pre_plane, jnp.zeros_like(pre_plane))
    hidden_blocks = hidden.reshape(row_count // 2, 2, col_count // 2, 2, channels)
    down_local = jnp.einsum(
        "ybxci,yxo->bcio", hidden_blocks, deep_grad, preferred_element_type=jnp.float32
    )
    slot_mask = (jnp.arange(2) == parity).astype(jnp.float32)
    down_terms = slot_mask[:, None, None, None, None] * down_local[None]
    grad_padded = extended(masked_grad[None], (("gz", 0), ("gy", 1)), 1)
    grad_padded = jnp.pad(grad_padded, ((0, 0), (0, 0), (1, 1), (0, 0)))
    input_padded = extended(level_input, (("gz", 0), ("gy", 1)), 1)
    input_padded = jnp.pad(input_padded, ((0, 0), (0, 0), (1, 1), (0, 0)))
    cell_count = row_count * col_count
    grad_flat = masked_grad.reshape(cell_count, channels)
    input_total = jnp.zeros((cell_count, channels), jnp.float32)
    conv_terms = []
    for kernel_z in range(3):
        grad_patches = jnp.concatenate(
            [
                grad_padded[
                    2 - kernel_z,
                    2 - kernel_y : 2 - kernel_y + row_count,
                    2 - kernel_x : 2 - kernel_x + col_count,
                    :,
                ]
                for kernel_y in range(3)
                for kernel_x in range(3)
            ],
            axis=-1,
        )
        grad_patches = grad_patches.reshape(cell_count, 9 * channels)
        conv_matrix = jnp.swapaxes(conv_weight[kernel_z], 2, 3).reshape(9 * channels, channels)
        input_total = input_total + jnp.dot(
            grad_patches, conv_matrix, preferred_element_type=jnp.float32
        )
        input_patches = jnp.concatenate(
            [
                input_padded[
                    kernel_z, kernel_y : kernel_y + row_count, kernel_x : kernel_x + col_count, :
                ]
                for kernel_y in range(3)
                for kernel_x in range(3)
            ],
            axis=-1,
        )
        input_patches = input_patches.reshape(cell_count, 9 * channels)
        slab_grad = lax.dot_general(
            input_patches, grad_flat, (((0,), (0,)), ((), ())), preferred_element_type=jnp.float32
        )
        slab_grad = slab_grad.reshape(3, 3, channels, channels)
        conv_terms.append(slab_grad)
    conv_local = jnp.stack(conv_terms)
    cell_total = lax.axis_size("gz") * lax.axis_size("gy") * cell_count
    conv_scale = math.sqrt(cell_total)
    down_scale = math.sqrt(cell_total // 8)
    conv_total, down_total = lax.psum((conv_local, down_terms), ("gz", "gy"))
    conv_weight_grad = (conv_total / conv_scale).astype(jnp.bfloat16)
    down_weight_grad = (down_total / down_scale).astype(jnp.bfloat16)
    input_grad = input_total.reshape(1, row_count, col_count, channels).astype(jnp.bfloat16)
    return (input_grad, conv_weight_grad, down_weight_grad)


def solution(mesh):
    return jax.shard_map(
        per_device,
        mesh=mesh,
        in_specs=(
            P("gz", "gy", None, None),
            P("gz", "gy", None, None),
            P(),
            P(),
            P("gz", "gy", None, None),
            P(None, "gy", None, "gz"),
        ),
        out_specs=(P("gz", "gy", None, None), P(), P()),
        check_vma=False,
    )
```

profile of v0, /device:TPU:1, one launch (start us, length us, event | category | flops | bytes accessed | tf_op | source)
XLA Modules:
  0.0 406.9 jit_solution(5054206653036867307)
XLA Ops:
  7.2 4.7 %collective-permute-start.5 = (bf16[1,8,64,128]{3,2,1,0:T(8,128)(2,1)}, bf16[1,8,64,128]{3,2,1,0:T(8,128)(2,1)S(1)}, u32[]{:S(2)}, u32[]{:S(2)}) collective-permute-start(bf16[1,8,64,128]{3,2,1,0:T(8,128)(2,1)} %param.6), channel_id=1, source_target_pairs={{0,4},{4,8},{8,12},{12,16},{16,20},{20,24},{24,28},{28,32},{32,36}... | collective-permute-start | bytes 393224 | tf_op jit(solution)/shard_map/ppermute | solution.py:21
  11.9 5.5 %collective-permute-start.6 = (bf16[1,8,64,128]{3,2,1,0:T(8,128)(2,1)}, bf16[1,8,64,128]{3,2,1,0:T(8,128)(2,1)S(1)}, u32[]{:S(2)}, u32[]{:S(2)}) collective-permute-start(bf16[1,8,64,128]{3,2,1,0:T(8,128)(2,1)} %param.6), channel_id=1, source_target_pairs={{4,0},{8,4},{12,8},{16,12},{20,16},{24,20},{28,24},{32,28},{36,32}... | collective-permute-start | bytes 393224 | tf_op jit(solution)/shard_map/ppermute | solution.py:23
  17.4 1.7 copy.37
  19.0 15.1 %all-to-all-start = ((bf16[128,2,32,2]{2,3,1,0:T(2,128)(2,1)}), bf16[128,2,32,2]{2,3,1,0:T(2,128)(2,1)S(1)}, u32[]{:S(2)}, u32[]{:S(2)}) async-start(bf16[128,2,32,2]{2,3,1,0:T(2,128)(2,1)} %bitcast.3), calls=%async_computation | async-start | bytes 262144 | tf_op jit(solution)/shard_map/all_to_all | solution.py:42
  34.2 1.2 fusion.13
  35.5 11.4 %all-to-all-done = bf16[128,2,32,2]{2,3,1,0:T(2,128)(2,1)S(1)} async-done(((bf16[128,2,32,2]{2,3,1,0:T(2,128)(2,1)}), bf16[128,2,32,2]{2,3,1,0:T(2,128)(2,1)S(1)}, u32[]{:S(2)}, u32[]{:S(2)}) %all-to-all-start) | async-done | bytes 32800 | tf_op jit(solution)/shard_map/all_to_all | solution.py:42
  47.1 2.3 collective-permute-start
  53.5 2.0 collective-permute-start.2
  55.5 3.5 collective-permute-start.1
  59.4 1.3 collective-permute-start.8
  60.7 4.0 collective-permute-start.7
  64.7 1.1 broadcast_multiply_fusion
  68.2 1.2 fusion.14
  71.1 1.7 pad_maximum_fusion.5
  72.8 1.7 copy.65
  74.5 1.7 copy.66
  76.2 1.7 copy.67
  77.8 1.7 copy.69
  79.5 1.7 copy.70
  81.1 1.7 copy.71
  84.4 1.7 copy.56
  98.6 1.7 copy.47
  100.3 1.7 copy.48
  102.0 1.7 copy.49
  103.6 1.7 copy.51
  106.1 1.7 copy.53
  112.9 1.3 collective-permute-start.4
  114.2 4.0 collective-permute-start.3
  118.2 1.4 pad_maximum_fusion
  123.5 1.1 fusion
  124.7 271.8 %all-reduce.5.cloned.1.call-done = (f32[3,3,3,128,128]{4,3,2,1,0:T(8,128)}, f32[2,2,2,128,256]{4,3,2,1,0:T(8,128)}) async-done(((f32[3,3,3,128,128]{4,3,2,1,0:T(8,128)}, f32[2,2,2,128,256]{4,3,2,1,0:T(8,128)}), (f32[3,3,3,128,128]{4,3,2,1,0:T(8,128)}, f32[2,2,2,128,256]{4,3,2,1,0:T(8,128)})) %all-reduce.5.cloned.1.call-update) | async-done | bytes 2818064 | tf_op jit(solution)/shard_map/psum | solution.py:112
  396.5 2.7 multiply_convert_fusion
  (160 shorter events, 33.0 us)
Async XLA Ops:
  7.2 45.8 %copy-start = (bf16[2,2,2,128,256]{4,3,2,1,0:T(8,128)(2,1)S(1)}, bf16[2,2,2,128,256]{4,3,2,1,0:T(8,128)(2,1)}, u32[]{:S(2)}) copy-start(bf16[2,2,2,128,256]{4,3,2,1,0:T(8,128)(2,1)} %param.9) | copy-start | bytes 1572868
  7.2 28.3 %copy-start.6 = (bf16[1,8,64,128]{3,2,1,0:T(8,128)(2,1)S(1)}, bf16[1,8,64,128]{3,2,1,0:T(8,128)(2,1)}, u32[]{:S(2)}) copy-start(bf16[1,8,64,128]{3,2,1,0:T(8,128)(2,1)} %param.7) | copy-start | bytes 393220
  7.2 52.1 %collective-permute-start.5 = (bf16[1,8,64,128]{3,2,1,0:T(8,128)(2,1)}, bf16[1,8,64,128]{3,2,1,0:T(8,128)(2,1)S(1)}, u32[]{:S(2)}, u32[]{:S(2)}) collective-permute-start(bf16[1,8,64,128]{3,2,1,0:T(8,128)(2,1)} %param.6), channel_id=1, source_target_pairs={{0,4},{4,8},{8,12},{12,16},{16,20},{20,24},{24,28},{28,32},{32,36}... | collective-permute-start | bytes 393224 | tf_op jit(solution)/shard_map/ppermute | solution.py:21
  11.9 47.4 %collective-permute-start.6 = (bf16[1,8,64,128]{3,2,1,0:T(8,128)(2,1)}, bf16[1,8,64,128]{3,2,1,0:T(8,128)(2,1)S(1)}, u32[]{:S(2)}, u32[]{:S(2)}) collective-permute-start(bf16[1,8,64,128]{3,2,1,0:T(8,128)(2,1)} %param.6), channel_id=1, source_target_pairs={{4,0},{8,4},{12,8},{16,12},{20,16},{24,20},{28,24},{32,28},{36,32}... | collective-permute-start | bytes 393224 | tf_op jit(solution)/shard_map/ppermute | solution.py:23
  19.0 27.9 %all-to-all-start = ((bf16[128,2,32,2]{2,3,1,0:T(2,128)(2,1)}), bf16[128,2,32,2]{2,3,1,0:T(2,128)(2,1)S(1)}, u32[]{:S(2)}, u32[]{:S(2)}) async-start(bf16[128,2,32,2]{2,3,1,0:T(2,128)(2,1)} %bitcast.3), calls=%async_computation | async-start | bytes 262144 | tf_op jit(solution)/shard_map/all_to_all | solution.py:42
  34.2 362.3 %all-reduce.5.cloned.1.call-start = ((), (), s32[]{:S(2)}) async-start(), calls=%async_computation.1 | async-start | bytes 5636096 | tf_op jit(solution)/shard_map/psum | solution.py:112
  35.5 16.6 %copy-start.10 = (bf16[1,8,64,128]{3,2,1,0:T(8,128)(2,1)S(1)}, bf16[1,8,64,128]{3,2,1,0:T(8,128)(2,1)}, u32[]{:S(2)}) copy-start(bf16[1,8,64,128]{3,2,1,0:T(8,128)(2,1)} %param.6) | copy-start | bytes 393220
  47.1 5.8 %collective-permute-start = (bf16[2,32,256]{2,1,0:T(8,128)(2,1)S(1)}, bf16[2,32,256]{2,1,0:T(8,128)(2,1)S(1)}, u32[]{:S(2)}, u32[]{:S(2)}) collective-permute-start(bf16[2,32,256]{2,1,0:T(8,128)(2,1)S(1)} %copy.40), channel_id=1, source_target_pairs={{0,4},{4,0},{8,12},{12,8},{16,20},{20,16},{24,28},{28,24},{32,36},... | collective-permute-start | bytes 98312 | tf_op jit(solution)/shard_map/ppermute | solution.py:10
  51.2 2.2 copy-start.25
  53.5 59.4 %collective-permute-start.2 = (bf16[1,8,64,128]{3,2,1,0:T(8,128)(2,1)S(1)}, bf16[1,8,64,128]{3,2,1,0:T(8,128)(2,1)S(1)}, u32[]{:S(2)}, u32[]{:S(2)}) collective-permute-start(bf16[1,8,64,128]{3,2,1,0:T(8,128)(2,1)S(1)} %select_convert_fusion), channel_id=1, source_target_pairs={{4,0},{8,4},{12,8},{16,12},{20,16},{24,20},{28,24},{32,28},{36,32}... | collective-permute-start | bytes 393224 | tf_op jit(solution)/shard_map/ppermute | solution.py:23
  55.5 57.4 %collective-permute-start.1 = (bf16[1,8,64,128]{3,2,1,0:T(8,128)(2,1)S(1)}, bf16[1,8,64,128]{3,2,1,0:T(8,128)(2,1)S(1)}, u32[]{:S(2)}, u32[]{:S(2)}) collective-permute-start(bf16[1,8,64,128]{3,2,1,0:T(8,128)(2,1)S(1)} %select_convert_fusion), channel_id=1, source_target_pairs={{0,4},{4,8},{8,12},{12,16},{16,20},{20,24},{24,28},{28,32},{32,36}... | collective-permute-start | bytes 393224 | tf_op jit(solution)/shard_map/ppermute | solution.py:21
  59.4 8.0 %collective-permute-start.8 = (bf16[3,1,64,128]{3,2,1,0:T(8,128)(2,1)S(1)}, bf16[3,1,64,128]{3,2,1,0:T(8,128)(2,1)S(1)}, u32[]{:S(2)}, u32[]{:S(2)}) collective-permute-start(bf16[3,1,64,128]{3,2,1,0:T(8,128)(2,1)S(1)} %get-tuple-element.60), channel_id=1, source_target_pairs={{1,0},{2,1},{3,2},{5,4},{6,5},{7,6},{9,8},{10,9},{11,10},{13,12},{... | collective-permute-start | bytes 147464 | tf_op jit(solution)/shard_map/ppermute | solution.py:23
  60.7 6.7 %collective-permute-start.7 = (bf16[3,1,64,128]{3,2,1,0:T(8,128)(2,1)S(1)}, bf16[3,1,64,128]{3,2,1,0:T(8,128)(2,1)S(1)}, u32[]{:S(2)}, u32[]{:S(2)}) collective-permute-start(bf16[3,1,64,128]{3,2,1,0:T(8,128)(2,1)S(1)} %get-tuple-element.59), channel_id=1, source_target_pairs={{0,1},{1,2},{2,3},{4,5},{5,6},{6,7},{8,9},{9,10},{10,11},{12,13},{... | collective-permute-start | bytes 147464 | tf_op jit(solution)/shard_map/ppermute | solution.py:21
  72.8 10.0 %copy-start.9 = (bf16[1,8,64,128]{3,2,1,0:T(8,128)(2,1)S(1)}, bf16[1,8,64,128]{3,2,1,0:T(8,128)(2,1)}, u32[]{:S(2)}) copy-start(bf16[1,8,64,128]{3,2,1,0:T(8,128)(2,1)} %get-tuple-element.25) | copy-start | bytes 393220
  72.8 10.8 %copy-start.8 = (bf16[1,8,64,128]{3,2,1,0:T(8,128)(2,1)S(1)}, bf16[1,8,64,128]{3,2,1,0:T(8,128)(2,1)}, u32[]{:S(2)}) copy-start(bf16[1,8,64,128]{3,2,1,0:T(8,128)(2,1)} %get-tuple-element.19) | copy-start | bytes 393220
  74.5 11.6 %copy-start.7 = (bf16[1,8,64,128]{3,2,1,0:T(8,128)(2,1)S(1)}, bf16[1,8,64,128]{3,2,1,0:T(8,128)(2,1)}, u32[]{:S(2)}) copy-start(bf16[1,8,64,128]{3,2,1,0:T(8,128)(2,1)} %get-tuple-element.18) | copy-start | bytes 393220
  86.0 7.0 %copy-start.13 = (bf16[512,128]{0,1:T(8,128)(2,1)S(1)}, bf16[512,128]{0,1:T(8,128)(2,1)}, u32[]{:S(2)}) copy-start(bf16[512,128]{0,1:T(8,128)(2,1)} %copy.68) | copy-start | bytes 393220
  88.3 6.6 %copy-start.20 = (bf16[512,128]{0,1:T(8,128)(2,1)S(1)}, bf16[512,128]{0,1:T(8,128)(2,1)}, u32[]{:S(2)}) copy-start(bf16[512,128]{0,1:T(8,128)(2,1)} %copy.71) | copy-start | bytes 393220
  89.1 5.8 %copy-start.17 = (bf16[512,128]{0,1:T(8,128)(2,1)S(1)}, bf16[512,128]{0,1:T(8,128)(2,1)}, u32[]{:S(2)}) copy-start(bf16[512,128]{0,1:T(8,128)(2,1)} %copy.72) | copy-start | bytes 393220
  94.9 1.3 copy-start.1
  94.9 1.3 copy-start.18
  95.0 1.3 copy-start.16
  95.0 1.3 copy-start.11
  95.0 1.3 copy-start.15
  95.0 1.4 copy-start.14
  106.1 5.3 %copy-start.12 = (bf16[512,128]{0,1:T(8,128)(2,1)S(1)}, bf16[512,128]{0,1:T(8,128)(2,1)}, u32[]{:S(2)}) copy-start(bf16[512,128]{0,1:T(8,128)(2,1)} %copy.50) | copy-start | bytes 393220
  108.5 3.8 copy-start.21
  108.5 3.8 copy-start.22
  108.5 3.8 copy-start.23
  112.9 6.7 %collective-permute-start.4 = (bf16[3,1,64,128]{3,2,1,0:T(8,128)(2,1)S(1)}, bf16[3,1,64,128]{3,2,1,0:T(8,128)(2,1)S(1)}, u32[]{:S(2)}, u32[]{:S(2)}) collective-permute-start(bf16[3,1,64,128]{3,2,1,0:T(8,128)(2,1)S(1)} %get-tuple-element.62), channel_id=1, source_target_pairs={{1,0},{2,1},{3,2},{5,4},{6,5},{7,6},{9,8},{10,9},{11,10},{13,12},{... | collective-permute-start | bytes 147464 | tf_op jit(solution)/shard_map/ppermute | solution.py:23
  114.2 5.4 %collective-permute-start.3 = (bf16[3,1,64,128]{3,2,1,0:T(8,128)(2,1)S(1)}, bf16[3,1,64,128]{3,2,1,0:T(8,128)(2,1)S(1)}, u32[]{:S(2)}, u32[]{:S(2)}) collective-permute-start(bf16[3,1,64,128]{3,2,1,0:T(8,128)(2,1)S(1)} %get-tuple-element.61), channel_id=1, source_target_pairs={{0,1},{1,2},{2,3},{4,5},{5,6},{6,7},{8,9},{9,10},{10,11},{12,13},{... | collective-permute-start | bytes 147464 | tf_op jit(solution)/shard_map/ppermute | solution.py:21
  396.5 2.7 copy-start.5
  (5 other events, 5.0 us)
Sparse Core Ops, SparseCore 0:
  119.7 276.7 all-reduce.4
where the time goes:
time: 408 us; the launch traced here: 407 us
  waiting for transfers between devices  283 us (69%)
  local copies, waits for them, and re-layouts  52.7 us (13%)
  starting transfers between devices  43.8 us (11%)
  between operations  14.9 us (4%)
  other arithmetic  8.36 us (2%)
    psum x1, waiting for transfers between devices, per_device(): conv_total, down_total = lax.psum((conv_local, down_terms), ('gz', 'gy'))  272 us
    concatenate x30, local copies, waits for them, and re-layouts, per_device(): jnp.concatenate([input_padded[kernel_z, kernel_y:kernel_y + row_count, ke...  30.7 us
    unnamed x106, local copies, waits for them, and re-layouts  18.6 us
    ppermute x4, starting transfers between devices, extended(): lax.ppermute(tail, axis, [(i, (i + 1) % count) for i in range(ends)])  16.2 us
    all_to_all x1, starting transfers between devices, per_device(): lax.all_to_all(halved, 'gz', split_axis=0, concat_axis=3, tiled=True)[0]  15.1 us
    all_to_all x1, waiting for transfers between devices, per_device(): lax.all_to_all(halved, 'gz', split_axis=0, concat_axis=3, tiled=True)[0]  11.4 us
    ppermute x4, starting transfers between devices, extended(): lax.ppermute(head, axis, [((i + 1) % count, i) for i in range(ends)])  10.1 us
  transfers between devices with their start and end apart: 11, of which 2 were waited for; matrix products, arithmetic and copies ran while one was open for 14% of the time, Pallas kernels for 0%

commit v1 on v0

--- a/solution.py
+++ b/solution.py
@@ -1,9 +1,291 @@
+import functools
 import math
 
 import jax
 import jax.numpy as jnp
 from jax import lax
+from jax.experimental import pallas as pl
+from jax.experimental.pallas import tpu as pltpu
 from jax.sharding import PartitionSpec as P
+
+MESH = pl.DeviceIdType.MESH
+TAPS = 27
+ROWS = 64
+LANES = 128
+BLOCKS = 44
+PARTS = (("x", "y", "z", 0, 20), ("y", "x", "z", 20, 12), ("z", "x", "y", 32, 12))
+
+
+def grid_sides(gz):
+    side = math.isqrt(gz // 2)
+    return side, side
+
+
+class Place:
+    def __init__(self, sizes):
+        self.n = sizes
+        gz = lax.axis_index("gz")
+        self.gz = gz
+        self.at = {
+            "z": gz // (2 * sizes["y"]),
+            "y": (gz // 2) % sizes["y"],
+            "c": gz % 2,
+            "x": lax.axis_index("gy"),
+        }
+
+    def peer(self, **moved):
+        at = dict(self.at, **moved)
+        return ((at["z"] * self.n["y"] + at["y"]) * 2 + at["c"], at["x"])
+
+    def ahead(self, axis, step):
+        return (self.at[axis] + step) % self.n[axis]
+
+    def behind(self, axis, step):
+        return (self.at[axis] + (self.n[axis] - step)) % self.n[axis]
+
+    def steps(self, axis):
+        count = self.n[axis]
+        return sorted(range(1, count), key=lambda d: -min(d, count - d))
+
+
+def remote(src, dst, sems, slot, device):
+    return pltpu.make_async_remote_copy(
+        src_ref=src,
+        dst_ref=dst,
+        send_sem=sems.at[0, slot],
+        recv_sem=sems.at[1, slot],
+        device_id=device,
+        device_id_type=MESH,
+    )
+
+
+def part_shapes(part, n):
+    a1, a2, a3, _, count = part
+    rows = ROWS // n["y"]
+    cut = count // n["x"]
+    piece = (cut, rows, LANES)
+    first = (cut, ROWS, LANES) if a1 == "x" else (count, rows, LANES)
+    return first, piece
+
+
+def part_scratch(part, n):
+    a1, a2, a3, _, _ = part
+    first, piece = part_shapes(part, n)
+    return [
+        pltpu.VMEM((n[a1],) + first, jnp.bfloat16),
+        pltpu.VMEM((n[a1],) + first, jnp.bfloat16),
+        pltpu.VMEM((n[a2],) + piece, jnp.float32),
+        pltpu.VMEM((n[a2],) + piece, jnp.float32),
+        pltpu.VMEM((n[a3],) + piece, jnp.float32),
+        pltpu.SemaphoreType.DMA((2, n[a1])),
+        pltpu.SemaphoreType.DMA((2, n[a2])),
+        pltpu.SemaphoreType.DMA((2, n[a3])),
+        pltpu.SemaphoreType.DMA((2, n[a2])),
+        pltpu.SemaphoreType.DMA((2, n[a1])),
+        pltpu.SemaphoreType.DMA((2, n[a1])),
+    ]
+
+
+PART_REFS = 11
+
+
+class PartSum:
+    def __init__(self, part, place, total, result, refs, scales):
+        self.a1, self.a2, self.a3, self.start, self.count = part
+        self.place = place
+        self.total = total
+        self.result = result
+        (self.out1, self.in1, self.out2, self.in2, self.all3) = refs[:5]
+        (self.s1, self.s2, self.s3, self.g2, self.g1, self.gc) = refs[5:]
+        self.rows = ROWS // place.n["y"]
+        self.cut = self.count // place.n["x"]
+        self.scales = scales
+        self.sent = []
+
+    def start_copy(self, copy):
+        copy.start()
+        self.sent.append(copy)
+
+    def span(self, ref, axes, where):
+        blocks = pl.ds(self.start, self.count)
+        rows = slice(None)
+        for axis in axes:
+            if axis == "x":
+                blocks = pl.ds(self.start + where["x"] * self.cut, self.cut)
+            else:
+                rows = pl.ds(pl.multiple_of(where[axis] * self.rows, self.rows), self.rows)
+        return ref.at[blocks, rows]
+
+    def scatter1(self):
+        place = self.place
+        for step in place.steps(self.a1):
+            to = place.ahead(self.a1, step)
+            self.out1[to] = self.span(self.total, (self.a1,), {self.a1: to})[...].astype(jnp.bfloat16)
+            self.start_copy(
+                remote(self.out1.at[to], self.in1.at[place.at[self.a1]], self.s1, step, place.peer(**{self.a1: to}))
+            )
+
+    def collect(self, held, sems, axis, first):
+        place = self.place
+        acc = first
+        for step in place.steps(axis)[::-1]:
+            source = place.behind(axis, step)
+            remote(held.at[source], held.at[source], sems, step, place.peer(**{axis: source})).wait_recv()
+            acc = acc + held[source].astype(jnp.float32)
+        return acc
+
+    def scatter2(self):
+        place = self.place
+        own = self.span(self.total, (self.a1,), place.at)[...]
+        acc = self.collect(self.in1, self.s1, self.a1, own)
+        for to in range(place.n[self.a2]):
+            if self.a2 == "x":
+                self.out2[to] = acc[to * self.cut : (to + 1) * self.cut]
+            else:
+                self.out2[to] = acc[:, to * self.rows : (to + 1) * self.rows]
+        for step in place.steps(self.a2):
+            to = place.ahead(self.a2, step)
+            self.start_copy(
+                remote(self.out2.at[to], self.in2.at[place.at[self.a2]], self.s2, step, place.peer(**{self.a2: to}))
+            )
+
+    def exchange3(self):
+        place = self.place
+        me = place.at[self.a3]
+        self.all3[me] = self.collect(self.in2, self.s2, self.a2, self.out2[place.at[self.a2]])
+        for step in place.steps(self.a3):
+            to = place.ahead(self.a3, step)
+            self.start_copy(remote(self.all3.at[me], self.all3.at[me], self.s3, step, place.peer(**{self.a3: to})))
+
+    def gather2(self):
+        place = self.place
+        for step in place.steps(self.a3)[::-1]:
+            source = place.behind(self.a3, step)
+            ref = self.all3.at[source]
+            remote(ref, ref, self.s3, step, place.peer(**{self.a3: source})).wait_recv()
+        acc = self.all3[0]
+        for source in range(1, place.n[self.a3]):
+            acc = acc + self.all3[source]
+        mine = self.span(self.result, (self.a1, self.a2), place.at)
+        conv_scale, down_scale = self.scales
+        block = self.start + place.at["x"] * self.cut
+        for i in range(self.cut):
+            scale = jnp.where(block + i < TAPS, jnp.float32(conv_scale), jnp.float32(down_scale))
+            mine[i] = (acc[i] / scale).astype(jnp.bfloat16)
+        for step in place.steps(self.a2):
+            to = place.ahead(self.a2, step)
+            self.start_copy(remote(mine, mine, self.g2, step, place.peer(**{self.a2: to})))
+
+    def gather1(self, partner_result):
+        place = self.place
+        for step in place.steps(self.a2)[::-1]:
+            source = place.behind(self.a2, step)
+            ref = self.span(self.result, (self.a1, self.a2), dict(place.at, **{self.a2: source}))
+            remote(ref, ref, self.g2, step, place.peer(**{self.a2: source})).wait_recv()
+        mine = self.span(self.result, (self.a1,), place.at)
+        for step in place.steps(self.a1):
+            to = place.ahead(self.a1, step)
+            self.start_copy(remote(mine, mine, self.g1, step, place.peer(**{self.a1: to})))
+        self.start_copy(remote(mine, mine, self.gc, 0, place.peer(c=1 - place.at["c"])))
+
+    def gather_core(self):
+        place = self.place
+        for step in place.steps(self.a1)[::-1]:
+            source = place.behind(self.a1, step)
+            ref = self.span(self.result, (self.a1,), {self.a1: source})
+            remote(ref, ref, self.g1, step, place.peer(**{self.a1: source})).wait_recv()
+            self.start_copy(remote(ref, ref, self.gc, step, place.peer(c=1 - place.at["c"])))
+
+    def finish(self, other):
+        place = self.place
+        for step in [0] + place.steps(self.a1)[::-1]:
+            source = place.behind(self.a1, step)
+            ref = self.span(other, (self.a1,), {self.a1: source})
+            remote(ref, ref, self.gc, step, place.peer(c=1 - place.at["c"])).wait_recv()
+        for copy in self.sent:
+            copy.wait_send()
+
+
+def store_results(result, conv_out, down_out, sems):
+    copies = []
+    for core in range(2):
+        copies.append(
+            pltpu.make_async_copy(result.at[core, pl.ds(0, TAPS)], conv_out.at[:, core], sems.at[3 * core])
+        )
+        for half in range(2):
+            for_half = result.at[core, pl.ds(TAPS + 8 * half, 8)]
+            copies.append(
+                pltpu.make_async_copy(
+                    for_half, down_out.at[core, :, :, pl.ds(LANES * half, LANES)], sems.at[3 * core + 1 + half]
+                )
+            )
+    for copy in copies:
+        copy.start()
+    for copy in copies:
+        copy.wait()
+
+
+def sum_kernel(n, scales, conv_ref, down_ref, conv_out, down_out, core_in, total, result, core_sems, out_sems, *refs):
+    place = Place(n)
+    core = place.at["c"]
+    barrier = pltpu.get_barrier_semaphore()
+    peers = [place.peer(c=1 - core)]
+    for axis in "xyz":
+        peers += [place.peer(**{axis: place.ahead(axis, step)}) for step in place.steps(axis)]
+    for device in peers:
+        pl.semaphore_signal(barrier, inc=1, device_id=device, device_id_type=MESH)
+    pl.semaphore_wait(barrier, len(peers))
+
+    swap = remote(conv_ref.at[:, 1 - core], core_in, core_sems, 0, place.peer(c=1 - core))
+    swap.start()
+    total[pl.ds(TAPS, 16)] = down_ref[...]
+    total[TAPS + 16] = jnp.zeros((ROWS, LANES), jnp.float32)
+    parts = []
+    for i, part in enumerate(PARTS):
+        parts.append(PartSum(part, place, total, result.at[core], refs[i * PART_REFS : (i + 1) * PART_REFS], scales))
+    parts[2].scatter1()
+    swap.wait_recv()
+    for tap in range(TAPS):
+        total[tap] = conv_ref[tap, core] + core_in[tap]
+    parts[1].scatter1()
+    parts[0].scatter1()
+    for stage in ("scatter2", "exchange3", "gather2"):
+        for part in parts[::-1]:
+            getattr(part, stage)()
+    for part in parts[::-1]:
+        part.gather1(None)
+    for part in parts[::-1]:
+        part.gather_core()
+    for part in parts[::-1]:
+        part.finish(result.at[1 - core])
+    swap.wait_send()
+    store_results(result, conv_out, down_out, out_sems)
+
+
+def sum_all(conv_local, down_local, sizes, scales):
+    scratch = [
+        pltpu.VMEM((TAPS, ROWS, LANES), jnp.float32),
+        pltpu.VMEM((BLOCKS, ROWS, LANES), jnp.float32),
+        pltpu.VMEM((2, BLOCKS, ROWS, LANES), jnp.bfloat16),
+        pltpu.SemaphoreType.DMA((2, 1)),
+        pltpu.SemaphoreType.DMA((6,)),
+    ]
+    for part in PARTS:
+        scratch += part_scratch(part, sizes)
+    conv_out, down_out = pl.pallas_call(
+        functools.partial(sum_kernel, sizes, scales),
+        out_shape=(
+            jax.ShapeDtypeStruct((TAPS, 2, ROWS, LANES), jnp.bfloat16),
+            jax.ShapeDtypeStruct((2, 8, ROWS, 2 * LANES), jnp.bfloat16),
+        ),
+        in_specs=[pl.BlockSpec(memory_space=pltpu.VMEM)] * 2,
+        out_specs=(pl.BlockSpec(memory_space=pl.ANY), pl.BlockSpec(memory_space=pl.ANY)),
+        scratch_shapes=scratch,
+        compiler_params=pltpu.CompilerParams(
+            collective_id=0, has_side_effects=True, vmem_limit_bytes=56 * 1024 * 1024
+        ),
+    )(conv_local, down_local)
+    return conv_out, down_out
 
 
 def swapped(array, axis, bit):
@@ -60,8 +342,7 @@
     down_local = jnp.einsum(
         "ybxci,yxo->bcio", hidden_blocks, deep_grad, preferred_element_type=jnp.float32
     )
-    slot_mask = (jnp.arange(2) == parity).astype(jnp.float32)
-    down_terms = slot_mask[:, None, None, None, None] * down_local[None]
+    down_blocks = down_local.reshape(8, ROWS, 2, LANES).transpose(2, 0, 1, 3).reshape(16, ROWS, LANES)
     grad_padded = extended(masked_grad[None], (("gz", 0), ("gy", 1)), 1)
     grad_padded = jnp.pad(grad_padded, ((0, 0), (0, 0), (1, 1), (0, 0)))
     input_padded = extended(level_input, (("gz", 0), ("gy", 1)), 1)
@@ -109,9 +390,12 @@
     cell_total = lax.axis_size("gz") * lax.axis_size("gy") * cell_count
     conv_scale = math.sqrt(cell_total)
     down_scale = math.sqrt(cell_total // 8)
-    conv_total, down_total = lax.psum((conv_local, down_terms), ("gz", "gy"))
-    conv_weight_grad = (conv_total / conv_scale).astype(jnp.bfloat16)
-    down_weight_grad = (down_total / down_scale).astype(jnp.bfloat16)
+    conv_local = conv_local.reshape(TAPS, 2, ROWS, LANES)
+    side_z, side_y = grid_sides(lax.axis_size("gz"))
+    sizes = {"z": side_z, "y": side_y, "x": lax.axis_size("gy"), "c": 2}
+    conv_weight_grad, down_weight_grad = sum_all(conv_local, down_blocks, sizes, (conv_scale, down_scale))
+    conv_weight_grad = conv_weight_grad.reshape(3, 3, 3, channels, channels)
+    down_weight_grad = down_weight_grad.reshape(2, 2, 2, channels, 2 * channels)
     input_grad = input_total.reshape(1, row_count, col_count, channels).astype(jnp.bfloat16)
     return (input_grad, conv_weight_grad, down_weight_grad)
 

time: 408 us -> 162 us (0.40)
  waiting for transfers between devices: 283 us -> 11.5 us
  Pallas kernels: 0 us -> 41.2 us
  between operations: 14.9 us -> 1.55 us
  other arithmetic: 8.36 us -> 3.64 us
    psum x1 -> x0, waiting for transfers between devices: 272 us -> none  [per_device(): conv_total, down_total = lax.psum((conv_local, down_terms), ('gz', 'gy'))]
    pallas_call x0 -> x1, Pallas kernels: none -> 41.2 us  [sum_all(): pl.pallas_call(functools.partial(sum_kernel, sizes, scales), out_shape=(j...]
    unnamed x106 -> x110, local copies, waits for them, and re-layouts: 18.6 us -> 20.3 us
  transfers between devices with their start and end apart: 11 -> 10, of which waited for: 2 -> 1; matrix products, arithmetic and copies ran while one was open for 14% -> 34% of each run, Pallas kernels for 0% -> 26%
where the time goes in v1:
time: 162 us; the launch traced here: 161 us
  local copies, waits for them, and re-layouts  55.2 us (34%)
  starting transfers between devices  44.1 us (27%)
  Pallas kernels  41.2 us (25%)
  waiting for transfers between devices  11.5 us (7%)
  matrix products  3.99 us (2%)
  other arithmetic  3.64 us (2%)
    pallas_call x1, Pallas kernels, sum_all(): pl.pallas_call(functools.partial(sum_kernel, sizes, scales), out_shape=(j...  41.2 us
    concatenate x30, local copies, waits for them, and re-layouts, per_device(): jnp.concatenate([input_padded[kernel_z, kernel_y:kernel_y + row_count, ke...  30.5 us
    unnamed x110, local copies, waits for them, and re-layouts  20.3 us
    ppermute x4, starting transfers between devices, extended(): lax.ppermute(tail, axis, [(i, (i + 1) % count) for i in range(ends)])  16.4 us
    all_to_all x1, starting transfers between devices, per_device(): lax.all_to_all(halved, 'gz', split_axis=0, concat_axis=3, tiled=True)[0]  15.3 us
    all_to_all x1, waiting for transfers between devices, per_device(): lax.all_to_all(halved, 'gz', split_axis=0, concat_axis=3, tiled=True)[0]  11.5 us
    ppermute x4, starting transfers between devices, extended(): lax.ppermute(head, axis, [((i + 1) % count, i) for i in range(ends)])  10.1 us
  transfers between devices with their start and end apart: 10, of which 1 were waited for; matrix products, arithmetic and copies ran while one was open for 34% of the time, Pallas kernels for 26%

profile of v1, /device:TPU:1, one launch (start us, length us, event | category | flops | bytes accessed | tf_op | source)
XLA Modules:
  0.0 161.2 jit_solution(11842363480520150454)
XLA Ops:
  0.6 4.7 %collective-permute-start.5 = (bf16[1,8,64,128]{3,2,1,0:T(8,128)(2,1)}, bf16[1,8,64,128]{3,2,1,0:T(8,128)(2,1)S(1)}, u32[]{:S(2)}, u32[]{:S(2)}) collective-permute-start(bf16[1,8,64,128]{3,2,1,0:T(8,128)(2,1)} %param.6), channel_id=1, source_target_pairs={{0,4},{4,8},{8,12},{12,16},{16,20},{20,24},{24,28},{28,32},{32,36}... | collective-permute-start | bytes 393224 | tf_op jit(solution)/shard_map/ppermute | solution.py:303
  5.4 5.5 %collective-permute-start.6 = (bf16[1,8,64,128]{3,2,1,0:T(8,128)(2,1)}, bf16[1,8,64,128]{3,2,1,0:T(8,128)(2,1)S(1)}, u32[]{:S(2)}, u32[]{:S(2)}) collective-permute-start(bf16[1,8,64,128]{3,2,1,0:T(8,128)(2,1)} %param.6), channel_id=1, source_target_pairs={{4,0},{8,4},{12,8},{16,12},{20,16},{24,20},{28,24},{32,28},{36,32}... | collective-permute-start | bytes 393224 | tf_op jit(solution)/shard_map/ppermute | solution.py:305
  10.8 1.7 %copy.38 = bf16[64,4,32,2]{2,3,1,0:T(2,128)(2,1)} copy(bf16[64,4,32,2]{0,3,2,1:T(2,128)(2,1)} %param.11) | data formatting | bytes 65536 | tf_op args[5]
  12.5 15.3 %all-to-all-start = ((bf16[128,2,32,2]{2,3,1,0:T(2,128)(2,1)}), bf16[128,2,32,2]{2,3,1,0:T(2,128)(2,1)S(1)}, u32[]{:S(2)}, u32[]{:S(2)}) async-start(bf16[128,2,32,2]{2,3,1,0:T(2,128)(2,1)} %bitcast.3), calls=%async_computation | async-start | bytes 262144 | tf_op jit(solution)/shard_map/all_to_all | solution.py:324
  27.8 1.2 fusion.15
  29.0 11.5 %all-to-all-done = bf16[128,2,32,2]{2,3,1,0:T(2,128)(2,1)S(1)} async-done(((bf16[128,2,32,2]{2,3,1,0:T(2,128)(2,1)}), bf16[128,2,32,2]{2,3,1,0:T(2,128)(2,1)S(1)}, u32[]{:S(2)}, u32[]{:S(2)}) %all-to-all-start) | async-done | bytes 32800 | tf_op jit(solution)/shard_map/all_to_all | solution.py:324
  40.7 2.3 %collective-permute-start = (bf16[2,32,256]{2,1,0:T(8,128)(2,1)S(1)}, bf16[2,32,256]{2,1,0:T(8,128)(2,1)S(1)}, u32[]{:S(2)}, u32[]{:S(2)}) collective-permute-start(bf16[2,32,256]{2,1,0:T(8,128)(2,1)S(1)} %copy.41), channel_id=1, source_target_pairs={{0,4},{4,0},{8,12},{12,8},{16,20},{20,16},{24,28},{28,24},{32,36},... | collective-permute-start | bytes 98312 | tf_op jit(solution)/shard_map/ppermute | solution.py:292
  47.3 2.0 %collective-permute-start.2 = (bf16[1,8,64,128]{3,2,1,0:T(8,128)(2,1)S(1)}, bf16[1,8,64,128]{3,2,1,0:T(8,128)(2,1)S(1)}, u32[]{:S(2)}, u32[]{:S(2)}) collective-permute-start(bf16[1,8,64,128]{3,2,1,0:T(8,128)(2,1)S(1)} %select_convert_fusion), channel_id=1, source_target_pairs={{4,0},{8,4},{12,8},{16,12},{20,16},{24,20},{28,24},{32,28},{36,32}... | collective-permute-start | bytes 393224 | tf_op jit(solution)/shard_map/ppermute | solution.py:305
  49.3 3.5 %collective-permute-start.1 = (bf16[1,8,64,128]{3,2,1,0:T(8,128)(2,1)S(1)}, bf16[1,8,64,128]{3,2,1,0:T(8,128)(2,1)S(1)}, u32[]{:S(2)}, u32[]{:S(2)}) collective-permute-start(bf16[1,8,64,128]{3,2,1,0:T(8,128)(2,1)S(1)} %select_convert_fusion), channel_id=1, source_target_pairs={{0,4},{4,8},{8,12},{12,16},{16,20},{20,24},{24,28},{28,32},{32,36}... | collective-permute-start | bytes 393224 | tf_op jit(solution)/shard_map/ppermute | solution.py:303
  53.0 1.3 collective-permute-start.8
  54.3 4.0 %collective-permute-start.7 = (bf16[3,1,64,128]{3,2,1,0:T(8,128)(2,1)S(1)}, bf16[3,1,64,128]{3,2,1,0:T(8,128)(2,1)S(1)}, u32[]{:S(2)}, u32[]{:S(2)}) collective-permute-start(bf16[3,1,64,128]{3,2,1,0:T(8,128)(2,1)S(1)} %get-tuple-element.61), channel_id=1, source_target_pairs={{0,1},{1,2},{2,3},{4,5},{5,6},{6,7},{8,9},{9,10},{10,11},{12,13},{... | collective-permute-start | bytes 147464 | tf_op jit(solution)/shard_map/ppermute | solution.py:303
  61.1 1.2 fusion.16
  64.0 1.7 %pad_maximum_fusion.5 = (bf16[1,8,64,128]{3,2,1,0:T(8,128)(2,1)}, bf16[1,8,64,128]{3,2,1,0:T(8,128)(2,1)}, bf16[1,8,64,128]{3,2,1,0:T(8,128)(2,1)}, bf16[1,8,64,...) fusion(bf16[3,1,64,128]{3,2,1,0:T(8,128)(2,1)S(1)} %collective-permute-done.8, ...), kind=kLoop, calls=%fused_computation.29 | loop fusion | flops 393216 | bytes 1277952 | tf_op jit(solution)/shard_map/slice | solution.py:375
  65.7 1.7 %copy.66 = bf16[512,128]{0,1:T(8,128)(2,1)} copy(bf16[512,128]{1,0:T(8,128)(2,1)} %bitcast.209) | data formatting | bytes 262144 | tf_op jit(solution)/shard_map/concatenate | solution.py:373
  67.4 1.7 %copy.67 = bf16[512,128]{0,1:T(8,128)(2,1)} copy(bf16[512,128]{1,0:T(8,128)(2,1)} %bitcast.198) | data formatting | bytes 262144 | tf_op jit(solution)/shard_map/concatenate | solution.py:373
  69.1 1.6 %copy.68 = bf16[512,128]{0,1:T(8,128)(2,1)} copy(bf16[512,128]{1,0:T(8,128)(2,1)} %bitcast.197) | data formatting | bytes 262144 | tf_op jit(solution)/shard_map/concatenate | solution.py:373
  70.8 1.7 %copy.70 = bf16[512,128]{0,1:T(8,128)(2,1)} copy(bf16[512,128]{1,0:T(8,128)(2,1)} %bitcast.194) | data formatting | bytes 262144 | tf_op jit(solution)/shard_map/concatenate | solution.py:373
  72.4 1.7 %copy.71 = bf16[512,128]{0,1:T(8,128)(2,1)} copy(bf16[512,128]{1,0:T(8,128)(2,1)} %bitcast.193) | data formatting | bytes 262144 | tf_op jit(solution)/shard_map/concatenate | solution.py:373
  74.1 1.7 %copy.72 = bf16[512,128]{0,1:T(8,128)(2,1)} copy(bf16[512,128]{1,0:T(8,128)(2,1)} %bitcast.208) | data formatting | bytes 262144 | tf_op jit(solution)/shard_map/concatenate | solution.py:373
  77.3 1.6 %copy.57 = bf16[512,128]{0,1:T(8,128)(2,1)} copy(bf16[512,128]{1,0:T(8,128)(2,1)} %bitcast.203) | data formatting | bytes 262144 | tf_op jit(solution)/shard_map/concatenate | solution.py:373
  82.0 1.0 copy.63
  91.5 1.7 %copy.48 = bf16[512,128]{0,1:T(8,128)(2,1)} copy(bf16[512,128]{1,0:T(8,128)(2,1)} %bitcast.171) | data formatting | bytes 262144 | tf_op jit(solution)/shard_map/concatenate | solution.py:373
  93.1 1.7 %copy.49 = bf16[512,128]{0,1:T(8,128)(2,1)} copy(bf16[512,128]{1,0:T(8,128)(2,1)} %bitcast.168) | data formatting | bytes 262144 | tf_op jit(solution)/shard_map/concatenate | solution.py:373
  94.8 1.7 %copy.50 = bf16[512,128]{0,1:T(8,128)(2,1)} copy(bf16[512,128]{1,0:T(8,128)(2,1)} %bitcast.167) | data formatting | bytes 262144 | tf_op jit(solution)/shard_map/concatenate | solution.py:373
  96.5 1.7 %copy.52 = bf16[512,128]{0,1:T(8,128)(2,1)} copy(bf16[512,128]{1,0:T(8,128)(2,1)} %bitcast.166) | data formatting | bytes 262144 | tf_op jit(solution)/shard_map/concatenate | solution.py:373
  98.9 1.7 %copy.54 = bf16[512,128]{0,1:T(8,128)(2,1)} copy(bf16[512,128]{1,0:T(8,128)(2,1)} %bitcast.170) | data formatting | bytes 262144 | tf_op jit(solution)/shard_map/concatenate | solution.py:373
  101.4 1.0 constant_dynamic-update-slice_fusion.37
  105.7 1.3 collective-permute-start.4
  107.0 4.2 %collective-permute-start.3 = (bf16[3,1,64,128]{3,2,1,0:T(8,128)(2,1)S(1)}, bf16[3,1,64,128]{3,2,1,0:T(8,128)(2,1)S(1)}, u32[]{:S(2)}, u32[]{:S(2)}) collective-permute-start(bf16[3,1,64,128]{3,2,1,0:T(8,128)(2,1)S(1)} %get-tuple-element.63), channel_id=1, source_target_pairs={{0,1},{1,2},{2,3},{4,5},{5,6},{6,7},{8,9},{9,10},{10,11},{12,13},{... | collective-permute-start | bytes 147464 | tf_op jit(solution)/shard_map/ppermute | solution.py:303
  111.2 1.4 pad_maximum_fusion
  112.5 41.2 %shard_map.85 = (bf16[27,2,64,128]{3,2,1,0:T(8,128)(2,1)}, bf16[2,8,64,256]{3,2,1,0:T(8,128)(2,1)}) custom-call(f32[27,2,64,128]{3,2,1,0:T(8,128)} %bitcast.151, f32[16,64,128]{2,1,0:T(8,128)} %bitcast.154), custom_call_target="tpu_custom_call" | custom-call | tf_op jit(solution)/shard_map/pallas_call | solution.py:275
  157.9 1.1 fusion
  (161 shorter events, 32.7 us)
Async XLA Ops:
  0.6 46.1 %copy-start = (bf16[2,2,2,128,256]{4,3,2,1,0:T(8,128)(2,1)S(1)}, bf16[2,2,2,128,256]{4,3,2,1,0:T(8,128)(2,1)}, u32[]{:S(2)}) copy-start(bf16[2,2,2,128,256]{4,3,2,1,0:T(8,128)(2,1)} %param.9) | copy-start | bytes 1572868
  0.6 52.2 %collective-permute-start.5 = (bf16[1,8,64,128]{3,2,1,0:T(8,128)(2,1)}, bf16[1,8,64,128]{3,2,1,0:T(8,128)(2,1)S(1)}, u32[]{:S(2)}, u32[]{:S(2)}) collective-permute-start(bf16[1,8,64,128]{3,2,1,0:T(8,128)(2,1)} %param.6), channel_id=1, source_target_pairs={{0,4},{4,8},{8,12},{12,16},{16,20},{20,24},{24,28},{28,32},{32,36}... | collective-permute-start | bytes 393224 | tf_op jit(solution)/shard_map/ppermute | solution.py:303
  5.4 47.6 %collective-permute-start.6 = (bf16[1,8,64,128]{3,2,1,0:T(8,128)(2,1)}, bf16[1,8,64,128]{3,2,1,0:T(8,128)(2,1)S(1)}, u32[]{:S(2)}, u32[]{:S(2)}) collective-permute-start(bf16[1,8,64,128]{3,2,1,0:T(8,128)(2,1)} %param.6), channel_id=1, source_target_pairs={{4,0},{8,4},{12,8},{16,12},{20,16},{24,20},{28,24},{32,28},{36,32}... | collective-permute-start | bytes 393224 | tf_op jit(solution)/shard_map/ppermute | solution.py:305
  12.5 30.5 %copy-start.6 = (bf16[1,8,64,128]{3,2,1,0:T(8,128)(2,1)S(1)}, bf16[1,8,64,128]{3,2,1,0:T(8,128)(2,1)}, u32[]{:S(2)}) copy-start(bf16[1,8,64,128]{3,2,1,0:T(8,128)(2,1)} %param.7) | copy-start | bytes 393220
  12.5 28.0 %all-to-all-start = ((bf16[128,2,32,2]{2,3,1,0:T(2,128)(2,1)}), bf16[128,2,32,2]{2,3,1,0:T(2,128)(2,1)S(1)}, u32[]{:S(2)}, u32[]{:S(2)}) async-start(bf16[128,2,32,2]{2,3,1,0:T(2,128)(2,1)} %bitcast.3), calls=%async_computation | async-start | bytes 262144 | tf_op jit(solution)/shard_map/all_to_all | solution.py:324
  40.6 5.2 %copy-start.11 = (bf16[1,8,64,128]{3,2,1,0:T(8,128)(2,1)S(1)}, bf16[1,8,64,128]{3,2,1,0:T(8,128)(2,1)}, u32[]{:S(2)}) copy-start(bf16[1,8,64,128]{3,2,1,0:T(8,128)(2,1)} %param.6) | copy-start | bytes 393220
  40.7 6.1 %collective-permute-start = (bf16[2,32,256]{2,1,0:T(8,128)(2,1)S(1)}, bf16[2,32,256]{2,1,0:T(8,128)(2,1)S(1)}, u32[]{:S(2)}, u32[]{:S(2)}) collective-permute-start(bf16[2,32,256]{2,1,0:T(8,128)(2,1)S(1)} %copy.41), channel_id=1, source_target_pairs={{0,4},{4,0},{8,12},{12,8},{16,20},{20,16},{24,28},{28,24},{32,36},... | collective-permute-start | bytes 98312 | tf_op jit(solution)/shard_map/ppermute | solution.py:292
  45.7 1.5 copy-start.26
  47.3 58.4 %collective-permute-start.2 = (bf16[1,8,64,128]{3,2,1,0:T(8,128)(2,1)S(1)}, bf16[1,8,64,128]{3,2,1,0:T(8,128)(2,1)S(1)}, u32[]{:S(2)}, u32[]{:S(2)}) collective-permute-start(bf16[1,8,64,128]{3,2,1,0:T(8,128)(2,1)S(1)} %select_convert_fusion), channel_id=1, source_target_pairs={{4,0},{8,4},{12,8},{16,12},{20,16},{24,20},{28,24},{32,28},{36,32}... | collective-permute-start | bytes 393224 | tf_op jit(solution)/shard_map/ppermute | solution.py:305
  49.3 56.4 %collective-permute-start.1 = (bf16[1,8,64,128]{3,2,1,0:T(8,128)(2,1)S(1)}, bf16[1,8,64,128]{3,2,1,0:T(8,128)(2,1)S(1)}, u32[]{:S(2)}, u32[]{:S(2)}) collective-permute-start(bf16[1,8,64,128]{3,2,1,0:T(8,128)(2,1)S(1)} %select_convert_fusion), channel_id=1, source_target_pairs={{0,4},{4,8},{8,12},{12,16},{16,20},{20,24},{24,28},{28,32},{32,36}... | collective-permute-start | bytes 393224 | tf_op jit(solution)/shard_map/ppermute | solution.py:303
  53.0 7.9 %collective-permute-start.8 = (bf16[3,1,64,128]{3,2,1,0:T(8,128)(2,1)S(1)}, bf16[3,1,64,128]{3,2,1,0:T(8,128)(2,1)S(1)}, u32[]{:S(2)}, u32[]{:S(2)}) collective-permute-start(bf16[3,1,64,128]{3,2,1,0:T(8,128)(2,1)S(1)} %get-tuple-element.62), channel_id=1, source_target_pairs={{1,0},{2,1},{3,2},{5,4},{6,5},{7,6},{9,8},{10,9},{11,10},{13,12},{... | collective-permute-start | bytes 147464 | tf_op jit(solution)/shard_map/ppermute | solution.py:305
  54.3 6.6 %collective-permute-start.7 = (bf16[3,1,64,128]{3,2,1,0:T(8,128)(2,1)S(1)}, bf16[3,1,64,128]{3,2,1,0:T(8,128)(2,1)S(1)}, u32[]{:S(2)}, u32[]{:S(2)}) collective-permute-start(bf16[3,1,64,128]{3,2,1,0:T(8,128)(2,1)S(1)} %get-tuple-element.61), channel_id=1, source_target_pairs={{0,1},{1,2},{2,3},{4,5},{5,6},{6,7},{8,9},{9,10},{10,11},{12,13},{... | collective-permute-start | bytes 147464 | tf_op jit(solution)/shard_map/ppermute | solution.py:303
  60.9 1.4 copy-start.25
  65.7 10.0 %copy-start.9 = (bf16[1,8,64,128]{3,2,1,0:T(8,128)(2,1)S(1)}, bf16[1,8,64,128]{3,2,1,0:T(8,128)(2,1)}, u32[]{:S(2)}) copy-start(bf16[1,8,64,128]{3,2,1,0:T(8,128)(2,1)} %get-tuple-element.27) | copy-start | bytes 393220
  65.7 10.8 %copy-start.8 = (bf16[1,8,64,128]{3,2,1,0:T(8,128)(2,1)S(1)}, bf16[1,8,64,128]{3,2,1,0:T(8,128)(2,1)}, u32[]{:S(2)}) copy-start(bf16[1,8,64,128]{3,2,1,0:T(8,128)(2,1)} %get-tuple-element.21) | copy-start | bytes 393220
  67.4 11.5 %copy-start.7 = (bf16[1,8,64,128]{3,2,1,0:T(8,128)(2,1)S(1)}, bf16[1,8,64,128]{3,2,1,0:T(8,128)(2,1)}, u32[]{:S(2)}) copy-start(bf16[1,8,64,128]{3,2,1,0:T(8,128)(2,1)} %get-tuple-element.20) | copy-start | bytes 393220
  78.9 7.0 %copy-start.14 = (bf16[512,128]{0,1:T(8,128)(2,1)S(1)}, bf16[512,128]{0,1:T(8,128)(2,1)}, u32[]{:S(2)}) copy-start(bf16[512,128]{0,1:T(8,128)(2,1)} %copy.69) | copy-start | bytes 393220
  81.2 6.6 %copy-start.21 = (bf16[512,128]{0,1:T(8,128)(2,1)S(1)}, bf16[512,128]{0,1:T(8,128)(2,1)}, u32[]{:S(2)}) copy-start(bf16[512,128]{0,1:T(8,128)(2,1)} %copy.72) | copy-start | bytes 393220
  82.0 5.8 %copy-start.18 = (bf16[512,128]{0,1:T(8,128)(2,1)S(1)}, bf16[512,128]{0,1:T(8,128)(2,1)}, u32[]{:S(2)}) copy-start(bf16[512,128]{0,1:T(8,128)(2,1)} %copy.73) | copy-start | bytes 393220
  87.8 1.3 copy-start.1
  87.8 1.3 copy-start.19
  87.9 1.3 copy-start.17
  87.9 1.3 copy-start.12
  87.9 1.3 copy-start.16
  87.9 1.4 copy-start.15
  98.9 5.3 %copy-start.13 = (bf16[512,128]{0,1:T(8,128)(2,1)S(1)}, bf16[512,128]{0,1:T(8,128)(2,1)}, u32[]{:S(2)}) copy-start(bf16[512,128]{0,1:T(8,128)(2,1)} %copy.51) | copy-start | bytes 393220
  101.4 3.8 %copy-start.22 = (bf16[512,128]{0,1:T(8,128)(2,1)S(1)}, bf16[512,128]{0,1:T(8,128)(2,1)}, u32[]{:S(2)}) copy-start(bf16[512,128]{0,1:T(8,128)(2,1)} %copy.53) | copy-start | bytes 393220
  101.4 3.8 %copy-start.23 = (bf16[512,128]{0,1:T(8,128)(2,1)S(1)}, bf16[512,128]{0,1:T(8,128)(2,1)}, u32[]{:S(2)}) copy-start(bf16[512,128]{0,1:T(8,128)(2,1)} %copy.54) | copy-start | bytes 393220
  101.4 3.8 %copy-start.24 = (bf16[512,128]{0,1:T(8,128)(2,1)S(1)}, bf16[512,128]{0,1:T(8,128)(2,1)}, u32[]{:S(2)}) copy-start(bf16[512,128]{0,1:T(8,128)(2,1)} %copy.55) | copy-start | bytes 393220
  105.7 48.0 %collective-permute-start.4 = (bf16[3,1,64,128]{3,2,1,0:T(8,128)(2,1)S(1)}, bf16[3,1,64,128]{3,2,1,0:T(8,128)(2,1)S(1)}, u32[]{:S(2)}, u32[]{:S(2)}) collective-permute-start(bf16[3,1,64,128]{3,2,1,0:T(8,128)(2,1)S(1)} %get-tuple-element.64), channel_id=1, source_target_pairs={{1,0},{2,1},{3,2},{5,4},{6,5},{7,6},{9,8},{10,9},{11,10},{13,12},{... | collective-permute-start | bytes 147464 | tf_op jit(solution)/shard_map/ppermute | solution.py:305
  107.0 46.8 %collective-permute-start.3 = (bf16[3,1,64,128]{3,2,1,0:T(8,128)(2,1)S(1)}, bf16[3,1,64,128]{3,2,1,0:T(8,128)(2,1)S(1)}, u32[]{:S(2)}, u32[]{:S(2)}) collective-permute-start(bf16[3,1,64,128]{3,2,1,0:T(8,128)(2,1)S(1)} %get-tuple-element.63), channel_id=1, source_target_pairs={{0,1},{1,2},{2,3},{4,5},{5,6},{6,7},{8,9},{9,10},{10,11},{12,13},{... | collective-permute-start | bytes 147464 | tf_op jit(solution)/shard_map/ppermute | solution.py:303
  159.1 1.4 copy-start.10
  (5 other events, 5.5 us)

commit v2 on v1

--- a/solution.py
+++ b/solution.py
@@ -225,30 +225,251 @@
         copy.wait()
 
 
-def sum_kernel(n, scales, conv_ref, down_ref, conv_out, down_out, core_in, total, result, core_sems, out_sems, *refs):
+SIDES = [(dz, dy) for dz in (1, -1, 0) for dy in (0, 1, -1) if (dz, dy) != (0, 0)]
+
+
+class Halo:
+    def __init__(self, place, counts, padded, sems):
+        self.place, self.counts, self.padded, self.sems = place, counts, padded, sems
+
+    def has(self, dz, dy):
+        z, y = self.place.gz + dz, self.place.at["x"] + dy
+        return (z >= 0) & (z < self.counts[0]) & (y >= 0) & (y < self.counts[1])
+
+    def copy(self, i, rows):
+        dz, dy = SIDES[i]
+        depth = rows.shape[0]
+        if dy == 0:
+            src, dst = rows, self.padded.at[1 - dz, pl.ds(1, depth)]
+        elif dy == 1:
+            src, dst = rows.at[pl.ds(depth - 1, 1)], self.padded.at[1 - dz, pl.ds(0, 1)]
+        else:
+            src, dst = rows.at[pl.ds(0, 1)], self.padded.at[1 - dz, pl.ds(depth + 1, 1)]
+        device = (self.place.gz + dz, self.place.at["x"] + dy)
+        return remote(src, dst, self.sems, i, device)
+
+    def clear(self):
+        depth = self.padded.shape[1] - 2
+        for dz, dy in SIDES:
+            rows = {0: pl.ds(1, depth), 1: pl.ds(0, 1), -1: pl.ds(depth + 1, 1)}[dy]
+
+            @pl.when(jnp.logical_not(self.has(-dz, -dy)))
+            def _():
+                window = self.padded.at[1 - dz, rows]
+                window[...] = jnp.zeros(window.shape, window.dtype)
+
+    def send(self, rows):
+        for i, side in enumerate(SIDES):
+            pl.when(self.has(*side))(self.copy(i, rows).start)
+
+    def receive(self, rows):
+        for i, (dz, dy) in enumerate(SIDES):
+            pl.when(self.has(-dz, -dy))(self.copy(i, rows).wait_recv)
+
+    def finish(self, rows):
+        for i, side in enumerate(SIDES):
+            pl.when(self.has(*side))(self.copy(i, rows).wait_send)
+
+
+def contract(a, b, dims):
+    return lax.dot_general(a, b, ((dims[:1], dims[1:]), ((), ())), preferred_element_type=jnp.float32)
+
+
+def shifted(values, column, count):
+    size = values.shape[0]
+    ahead = jnp.where(column == count - 1, 0.0, pltpu.roll(values, size - 1, 0))
+    behind = jnp.where(column == 0, 0.0, pltpu.roll(values, 1, 0))
+    return ahead, behind
+
+
+def bits(value, start, width):
+    return lax.shift_right_logical(value, start) & ((1 << width) - 1)
+
+
+def level_kernel(
+    n,
+    counts,
+    scales,
+    level_ref,
+    pre_ref,
+    weight_ref,
+    down_ref,
+    skip_ref,
+    deep_ref,
+    input_out,
+    conv_out,
+    down_out,
+    order,
+    deep_in,
+    deep_sorted,
+    deep_all,
+    level_pad,
+    grad_pad,
+    grad_wide,
+    input_sum,
+    input_rows,
+    conv_local,
+    core_in,
+    total,
+    result,
+    deep_sems,
+    plane_sems,
+    level_sems,
+    grad_sems,
+    core_sems,
+    out_sems,
+    *refs,
+):
     place = Place(n)
     core = place.at["c"]
+    partner = place.peer(c=1 - core)
+    rows, cols = level_ref.shape[0], level_ref.shape[1]
+    half = rows // 2 * cols
+    level_halo = Halo(place, counts, level_pad, level_sems)
+    grad_halo = Halo(place, counts, grad_pad, grad_sems)
+
     barrier = pltpu.get_barrier_semaphore()
-    peers = [place.peer(c=1 - core)]
+    peers = [partner]
     for axis in "xyz":
         peers += [place.peer(**{axis: place.ahead(axis, step)}) for step in place.steps(axis)]
+    peers += [place.peer(y=place.ahead("y", step), c=1 - core) for step in place.steps("y")]
     for device in peers:
         pl.semaphore_signal(barrier, inc=1, device_id=device, device_id_type=MESH)
-    pl.semaphore_wait(barrier, len(peers))
-
-    swap = remote(conv_ref.at[:, 1 - core], core_in, core_sems, 0, place.peer(c=1 - core))
-    swap.start()
-    total[pl.ds(TAPS, 16)] = down_ref[...]
-    total[TAPS + 16] = jnp.zeros((ROWS, LANES), jnp.float32)
+    arrivals = len(peers)
+    for dz, dy in SIDES:
+        near = level_halo.has(dz, dy)
+        arrivals = arrivals + near.astype(jnp.int32)
+
+        @pl.when(near)
+        def _():
+            device = (place.gz + dz, place.at["x"] + dy)
+            pl.semaphore_signal(barrier, inc=1, device_id=device, device_id_type=MESH)
+
+    wide = order.shape[0]
+    share_bits = (deep_ref.shape[1] // n["z"]).bit_length() - 1
+    y_bits, z_bits = n["y"].bit_length() - 1, n["z"].bit_length() - 1
+    row = lax.broadcasted_iota(jnp.int32, (wide, wide), 0)
+    col = lax.broadcasted_iota(jnp.int32, (wide, wide), 1)
+    low = bits(row, 0, share_bits)
+    source = bits(row, share_bits, 1 + y_bits)
+    target = bits(row, share_bits + 1 + y_bits, z_bits)
+    wanted = ((source << z_bits) + target << share_bits) + low
+    order[...] = jnp.where(col == wanted, 1.0, 0.0).astype(jnp.bfloat16)
+    level_halo.clear()
+    grad_halo.clear()
+    level_pad[1, pl.ds(1, rows)] = level_ref[...]
+    total[BLOCKS - 1] = jnp.zeros((ROWS, LANES), jnp.float32)
+    me_y, me_z = place.at["y"], place.at["z"]
+    deep_in[me_y, core] = deep_ref[me_y]
+    pl.semaphore_wait(barrier, arrivals)
+
+    sent = []
+    first = []
+    for step in place.steps("y") + [0]:
+        to = place.ahead("y", step)
+        for cross in range(2):
+            if step == 0 and cross == 0:
+                continue
+            there = 1 - core if cross else core
+            copy = remote(
+                deep_ref.at[to], deep_in.at[me_y, core], deep_sems, 2 * step + cross, place.peer(y=to, c=there)
+            )
+            copy.start()
+            sent.append(copy)
+            first.append((step, cross))
+    level_halo.send(level_ref)
+    for step, cross in first[::-1]:
+        origin = place.behind("y", step)
+        window = deep_in.at[origin, 1 - core if cross else core]
+        remote(window, window, deep_sems, 2 * step + cross, partner).wait_recv()
+    held = deep_in[...].reshape(wide, half // 2)
+    deep_sorted[...] = contract(order[...], held, (1, 0)).astype(jnp.bfloat16).reshape(deep_sorted.shape)
+    for step in place.steps("z"):
+        to = place.ahead("z", step)
+        copy = remote(deep_sorted.at[to], deep_all.at[me_z], plane_sems, step, place.peer(z=to))
+        copy.start()
+        sent.append(copy)
+    deep_all[me_z] = deep_sorted[me_z]
+    for step in place.steps("z")[::-1]:
+        window = deep_all.at[place.behind("z", step)]
+        remote(window, window, plane_sems, step, partner).wait_recv()
+
+    cell = lax.broadcasted_iota(jnp.int32, (half, half // 2), 0)
+    deep_cell = lax.broadcasted_iota(jnp.int32, (half, half // 2), 1)
+    spread = jnp.where(lax.shift_right_logical(cell, 1) == deep_cell, 1.0, 0.0).astype(jnp.bfloat16)
+    deep = deep_all[...].reshape(wide, half // 2)
+    covering = contract(spread, deep, (1, 1)).astype(jnp.bfloat16)
+    column = lax.broadcasted_iota(jnp.int32, (half, LANES), 0) & (cols - 1)
+    odd = (column & 1) == 1
+    down = contract(covering, down_ref[core], (1, 1))
+    for b in range(2):
+        even_part = down[:, 2 * b * LANES : (2 * b + 1) * LANES]
+        odd_part = down[:, (2 * b + 1) * LANES : (2 * b + 2) * LANES]
+        grad = jnp.where(odd, odd_part, even_part) + skip_ref[:, b].reshape(half, LANES).astype(jnp.float32)
+        grad = jnp.where(pre_ref[:, b].reshape(half, LANES) > 0, grad, 0.0)
+        ahead, behind = shifted(grad, column, cols)
+        for y in range(rows // 2):
+            span = slice(y * cols, (y + 1) * cols)
+            grad_pad[1, 1 + 2 * y + b] = grad[span].astype(jnp.bfloat16)
+            grad_wide[2 * y + b, :, 0:LANES] = ahead[span].astype(jnp.bfloat16)
+            grad_wide[2 * y + b, :, LANES : 2 * LANES] = grad[span].astype(jnp.bfloat16)
+            grad_wide[2 * y + b, :, 2 * LANES :] = behind[span].astype(jnp.bfloat16)
+    own_rows = grad_pad.at[1, pl.ds(1, rows)]
+    grad_halo.send(own_rows)
+
+    grads = grad_wide[...].reshape(rows * cols, 3 * LANES)
+    swaps = [None] * 3
+    for kz in (1, 0, 2):
+        if kz == 1:
+            level_halo.receive(level_ref)
+        for ky in range(3):
+            cells = level_pad[kz, pl.ds(ky, rows)].reshape(rows * cols, LANES)
+            slab = contract(cells, grads, (0, 0))
+            for kx in range(3):
+                for part in range(2):
+                    conv_local[kz, part, 3 * ky + kx] = slab[
+                        part * ROWS : (part + 1) * ROWS, kx * LANES : (kx + 1) * LANES
+                    ]
+        swaps[kz] = remote(conv_local.at[kz, 1 - core], core_in.at[kz], core_sems, kz, partner)
+        swaps[kz].start()
+    for b in range(2):
+        hidden = jnp.maximum(pre_ref[:, b].reshape(half, LANES).astype(jnp.float32), 0.0)
+        pair = jnp.concatenate([jnp.where(odd, 0.0, hidden), jnp.where(odd, hidden, 0.0)], axis=1)
+        slab = contract(pair.astype(jnp.bfloat16), covering, (0, 0))
+        for c in range(2):
+            for part in range(2):
+                for side in range(2):
+                    total[TAPS + 8 * side + 2 * (2 * b + c) + part] = slab[
+                        c * LANES + part * ROWS : c * LANES + (part + 1) * ROWS, side * LANES : (side + 1) * LANES
+                    ]
+
     parts = []
     for i, part in enumerate(PARTS):
         parts.append(PartSum(part, place, total, result.at[core], refs[i * PART_REFS : (i + 1) * PART_REFS], scales))
     parts[2].scatter1()
-    swap.wait_recv()
-    for tap in range(TAPS):
-        total[tap] = conv_ref[tap, core] + core_in[tap]
+    for kz in (1, 0, 2):
+        swaps[kz].wait_recv()
+        for tap in range(9):
+            total[9 * kz + tap] = conv_local[kz, core, tap] + core_in[kz, tap]
     parts[1].scatter1()
     parts[0].scatter1()
+
+    grad_halo.receive(own_rows)
+    for kz in range(3):
+        acc = None
+        for ky in range(3):
+            cells = grad_pad[2 - kz, pl.ds(2 - ky, rows)].reshape(rows * cols, LANES)
+            term = contract(cells, weight_ref[3 * kz + ky], (1, 1))
+            acc = term if acc is None else acc + term
+        input_sum[...] = acc if kz == 0 else input_sum[...] + acc
+    column = lax.broadcasted_iota(jnp.int32, (rows * cols, LANES), 0) & (cols - 1)
+    ahead, _ = shifted(input_sum[:, 0:LANES], column, cols)
+    _, behind = shifted(input_sum[:, 2 * LANES :], column, cols)
+    sums = input_sum[:, LANES : 2 * LANES] + ahead + behind
+    input_rows[...] = sums.astype(jnp.bfloat16).reshape(input_rows.shape)
+    input_copy = pltpu.make_async_copy(input_rows, input_out, out_sems.at[6])
+    input_copy.start()
+
     for stage in ("scatter2", "exchange3", "gather2"):
         for part in parts[::-1]:
             getattr(part, stage)()
@@ -258,146 +479,77 @@
         part.gather_core()
     for part in parts[::-1]:
         part.finish(result.at[1 - core])
-    swap.wait_send()
+    for copy in sent + swaps:
+        copy.wait_send()
+    level_halo.finish(level_ref)
+    grad_halo.finish(own_rows)
+    input_copy.wait()
     store_results(result, conv_out, down_out, out_sems)
 
 
-def sum_all(conv_local, down_local, sizes, scales):
+def per_device(level_input, pre_activation, conv_weight, down_weight, skip_cotangent, deep_cotangent):
+    rows, cols, channels = level_input.shape[1:]
+    planes, deep_rows, deep_cols, share = deep_cotangent.shape
+    counts = (lax.axis_size("gz"), lax.axis_size("gy"))
+    side_z, side_y = grid_sides(counts[0])
+    n = {"z": side_z, "y": side_y, "x": counts[1], "c": 2}
+    cell_count = rows * cols
+    cell_total = counts[0] * counts[1] * cell_count
+    scales = (math.sqrt(cell_total), math.sqrt(cell_total // 8))
+    deep_cells = deep_rows * deep_cols
+    wide = counts[0] * share
+    messages = deep_cotangent.reshape(side_z, side_y, deep_cells, share).transpose(1, 0, 3, 2)
+    messages = messages.reshape(side_y, side_z * share, deep_cells)
+    pad = (3, rows + 2, cols, channels)
     scratch = [
-        pltpu.VMEM((TAPS, ROWS, LANES), jnp.float32),
+        pltpu.VMEM((wide, wide), jnp.bfloat16),
+        pltpu.VMEM((side_y, 2, side_z * share, deep_cells), jnp.bfloat16),
+        pltpu.VMEM((side_z, side_y * 2 * share, deep_cells), jnp.bfloat16),
+        pltpu.VMEM((side_z, side_y * 2 * share, deep_cells), jnp.bfloat16),
+        pltpu.VMEM(pad, jnp.bfloat16),
+        pltpu.VMEM(pad, jnp.bfloat16),
+        pltpu.VMEM((rows, cols, 3 * channels), jnp.bfloat16),
+        pltpu.VMEM((cell_count, 3 * channels), jnp.float32),
+        pltpu.VMEM((rows, cols, channels), jnp.bfloat16),
+        pltpu.VMEM((3, 2, 9, ROWS, LANES), jnp.float32),
+        pltpu.VMEM((3, 9, ROWS, LANES), jnp.float32),
         pltpu.VMEM((BLOCKS, ROWS, LANES), jnp.float32),
         pltpu.VMEM((2, BLOCKS, ROWS, LANES), jnp.bfloat16),
-        pltpu.SemaphoreType.DMA((2, 1)),
-        pltpu.SemaphoreType.DMA((6,)),
+        pltpu.SemaphoreType.DMA((2, 2 * side_y)),
+        pltpu.SemaphoreType.DMA((2, side_z)),
+        pltpu.SemaphoreType.DMA((2, len(SIDES))),
+        pltpu.SemaphoreType.DMA((2, len(SIDES))),
+        pltpu.SemaphoreType.DMA((2, 3)),
+        pltpu.SemaphoreType.DMA((7,)),
     ]
     for part in PARTS:
-        scratch += part_scratch(part, sizes)
-    conv_out, down_out = pl.pallas_call(
-        functools.partial(sum_kernel, sizes, scales),
+        scratch += part_scratch(part, n)
+    input_grad, conv_grad, down_grad = pl.pallas_call(
+        functools.partial(level_kernel, n, counts, scales),
         out_shape=(
+            jax.ShapeDtypeStruct((rows, cols, channels), jnp.bfloat16),
             jax.ShapeDtypeStruct((TAPS, 2, ROWS, LANES), jnp.bfloat16),
             jax.ShapeDtypeStruct((2, 8, ROWS, 2 * LANES), jnp.bfloat16),
         ),
-        in_specs=[pl.BlockSpec(memory_space=pltpu.VMEM)] * 2,
-        out_specs=(pl.BlockSpec(memory_space=pl.ANY), pl.BlockSpec(memory_space=pl.ANY)),
+        in_specs=[pl.BlockSpec(memory_space=pltpu.VMEM)] * 6,
+        out_specs=[pl.BlockSpec(memory_space=pl.ANY)] * 3,
         scratch_shapes=scratch,
         compiler_params=pltpu.CompilerParams(
             collective_id=0, has_side_effects=True, vmem_limit_bytes=56 * 1024 * 1024
         ),
-    )(conv_local, down_local)
-    return conv_out, down_out
-
-
-def swapped(array, axis, bit):
-    return lax.ppermute(array, axis, [(i, i ^ 1 << bit) for i in range(lax.axis_size(axis))])
-
-
-def extended(cells, sides, width):
-    for axis, dim in sides:
-        count = lax.axis_size(axis)
-        ends = count - 1
-        head = lax.slice_in_dim(cells, 0, width, axis=dim)
-        tail = lax.slice_in_dim(cells, cells.shape[dim] - width, cells.shape[dim], axis=dim)
-        cells = jnp.concatenate(
-            [
-                lax.ppermute(tail, axis, [(i, (i + 1) % count) for i in range(ends)]),
-                cells,
-                lax.ppermute(head, axis, [((i + 1) % count, i) for i in range(ends)]),
-            ],
-            axis=dim,
-        )
-    return cells
-
-
-def per_device(
-    level_input, pre_activation, conv_weight, down_weight, skip_cotangent, deep_cotangent
-):
-    row_count = level_input.shape[1]
-    col_count = level_input.shape[2]
-    channels = level_input.shape[3]
-    plane_count = deep_cotangent.shape[0]
-    deep_rows = deep_cotangent.shape[1]
-    deep_cols = deep_cotangent.shape[2]
-    deep_share = deep_cotangent.shape[3]
-    parity = lax.axis_index("gz") % 2
-    halved = deep_cotangent.reshape(2 * plane_count, deep_rows // 2, deep_cols, deep_share)
-    own_half = lax.all_to_all(halved, "gz", split_axis=0, concat_axis=3, tiled=True)[0]
-    pair_half = swapped(own_half, "gz", 0)
-    even_plane = parity == 0
-    top_half = jnp.where(even_plane, own_half, pair_half)
-    low_half = jnp.where(even_plane, pair_half, own_half)
-    deep_grad = jnp.concatenate([top_half, low_half], axis=0)
-    down_slice = lax.dynamic_index_in_dim(down_weight, parity, 0, keepdims=False)
-    down_part = jnp.einsum(
-        "yxo,bcio->ybxci", deep_grad, down_slice, preferred_element_type=jnp.float32
+    )(
+        level_input.reshape(rows, cols, channels),
+        pre_activation.reshape(rows // 2, 2, cols, channels),
+        conv_weight.reshape(9, 3 * channels, channels),
+        down_weight.reshape(2, 4 * channels, 2 * channels),
+        skip_cotangent.reshape(rows // 2, 2, cols, channels),
+        messages,
     )
-    down_part = down_part.reshape(row_count, col_count, channels)
-    hidden_grad = down_part + skip_cotangent[0].astype(jnp.float32)
-    pre_plane = pre_activation[0]
-    masked_grad = jnp.where(pre_plane > 0, hidden_grad, jnp.zeros_like(hidden_grad)).astype(
-        jnp.bfloat16
+    return (
+        input_grad.reshape(1, rows, cols, channels),
+        conv_grad.reshape(3, 3, 3, channels, channels),
+        down_grad.reshape(2, 2, 2, channels, 2 * channels),
     )
-    hidden = jnp.maximum(pre_plane, jnp.zeros_like(pre_plane))
-    hidden_blocks = hidden.reshape(row_count // 2, 2, col_count // 2, 2, channels)
-    down_local = jnp.einsum(
-        "ybxci,yxo->bcio", hidden_blocks, deep_grad, preferred_element_type=jnp.float32
-    )
-    down_blocks = down_local.reshape(8, ROWS, 2, LANES).transpose(2, 0, 1, 3).reshape(16, ROWS, LANES)
-    grad_padded = extended(masked_grad[None], (("gz", 0), ("gy", 1)), 1)
-    grad_padded = jnp.pad(grad_padded, ((0, 0), (0, 0), (1, 1), (0, 0)))
-    input_padded = extended(level_input, (("gz", 0), ("gy", 1)), 1)
-    input_padded = jnp.pad(input_padded, ((0, 0), (0, 0), (1, 1), (0, 0)))
-    cell_count = row_count * col_count
-    grad_flat = masked_grad.reshape(cell_count, channels)
-    input_total = jnp.zeros((cell_count, channels), jnp.float32)
-    conv_terms = []
-    for kernel_z in range(3):
-        grad_patches = jnp.concatenate(
-            [
-                grad_padded[
-                    2 - kernel_z,
-                    2 - kernel_y : 2 - kernel_y + row_count,
-                    2 - kernel_x : 2 - kernel_x + col_count,
-                    :,
-                ]
-                for kernel_y in range(3)
-                for kernel_x in range(3)
-            ],
-            axis=-1,
-        )
-        grad_patches = grad_patches.reshape(cell_count, 9 * channels)
-        conv_matrix = jnp.swapaxes(conv_weight[kernel_z], 2, 3).reshape(9 * channels, channels)
-        input_total = input_total + jnp.dot(
-            grad_patches, conv_matrix, preferred_element_type=jnp.float32
-        )
-        input_patches = jnp.concatenate(
-            [
-                input_padded[
-                    kernel_z, kernel_y : kernel_y + row_count, kernel_x : kernel_x + col_count, :
-                ]
-                for kernel_y in range(3)
-                for kernel_x in range(3)
-            ],
-            axis=-1,
-        )
-        input_patches = input_patches.reshape(cell_count, 9 * channels)
-        slab_grad = lax.dot_general(
-            input_patches, grad_flat, (((0,), (0,)), ((), ())), preferred_element_type=jnp.float32
-        )
-        slab_grad = slab_grad.reshape(3, 3, channels, channels)
-        conv_terms.append(slab_grad)
-    conv_local = jnp.stack(conv_terms)
-    cell_total = lax.axis_size("gz") * lax.axis_size("gy") * cell_count
-    conv_scale = math.sqrt(cell_total)
-    down_scale = math.sqrt(cell_total // 8)
-    conv_local = conv_local.reshape(TAPS, 2, ROWS, LANES)
-    side_z, side_y = grid_sides(lax.axis_size("gz"))
-    sizes = {"z": side_z, "y": side_y, "x": lax.axis_size("gy"), "c": 2}
-    conv_weight_grad, down_weight_grad = sum_all(conv_local, down_blocks, sizes, (conv_scale, down_scale))
-    conv_weight_grad = conv_weight_grad.reshape(3, 3, 3, channels, channels)
-    down_weight_grad = down_weight_grad.reshape(2, 2, 2, channels, 2 * channels)
-    input_grad = input_total.reshape(1, row_count, col_count, channels).astype(jnp.bfloat16)
-    return (input_grad, conv_weight_grad, down_weight_grad)
 
 
 def solution(mesh):

time: 162 us -> 71.5 us (0.44)
  local copies, waits for them, and re-layouts: 55.2 us -> 6.38 us
  starting transfers between devices: 44.1 us -> 0 us
  Pallas kernels: 41.2 us -> 64.2 us
  waiting for transfers between devices: 11.5 us -> 0 us
  matrix products: 3.99 us -> 0 us
  other arithmetic: 3.64 us -> 0 us
    concatenate x34 -> x0, local copies, waits for them, and re-layouts: 30.6 us -> none  [the longest x30 30.5 us: per_device(): jnp.concatenate([input_padded[kernel_z, kernel_y:kernel_y + row_count, ke...]
    ppermute x9 -> x0, starting transfers between devices: 28.8 us -> none  [the longest x4 16.4 us: extended(): lax.ppermute(tail, axis, [(i, (i + 1) % count) for i in range(ends)])]
    pallas_call x1, Pallas kernels: 41.2 us -> 64.2 us  [per_device(): pl.pallas_call(functools.partial(level_kernel, n, counts, scales), out_sh...]
    all_to_all x1 -> x0, starting transfers between devices: 15.3 us -> none  [per_device(): lax.all_to_all(halved, 'gz', split_axis=0, concat_axis=3, tiled=True)[0]]
    unnamed x110 -> x6, local copies, waits for them, and re-layouts: 20.3 us -> 5.6 us
    all_to_all x1 -> x0, waiting for transfers between devices: 11.5 us -> none  [per_device(): lax.all_to_all(halved, 'gz', split_axis=0, concat_axis=3, tiled=True)[0]]
    dot_general x8 -> x0, matrix products: 3.99 us -> none  [the longest x3 2.09 us: per_device(): jnp.dot(grad_patches, conv_matrix, preferred_element_type=jnp.float32)]
    slice x4 -> x0, local copies, waits for them, and re-layouts: 2.91 us -> none  [the longest x1 1.21 us: per_device(): input_padded[kernel_z, kernel_y:kernel_y + row_count, kernel_x:kernel_x +...]
  transfers between devices with their start and end apart: 10 -> 0, of which waited for: 1 -> 0; matrix products, arithmetic and copies ran while one was open for 34% -> 0% of each run, Pallas kernels for 26% -> 0%
where the time goes in v2:
time: 71.5 us; the launch traced here: 71.2 us
  Pallas kernels  64.2 us (90%)
  local copies, waits for them, and re-layouts  6.38 us (9%)
    pallas_call x1, Pallas kernels, per_device(): pl.pallas_call(functools.partial(level_kernel, n, counts, scales), out_sh...  64.2 us
    unnamed x6, local copies, waits for them, and re-layouts  5.6 us

profile of v2, /device:TPU:1, one launch (start us, length us, event | category | flops | bytes accessed | tf_op | source)
XLA Modules:
  0.0 71.2 jit_solution(12827161268354967806)
XLA Ops:
  0.6 1.0 %copy.10 = bf16[64,4,32,2]{2,1,0,3:T(4,128)(2,1)S(1)} copy(bf16[64,4,32,2]{0,3,2,1:T(2,128)(2,1)} %param.11) | data formatting | bytes 65536 | tf_op args[5]
  1.6 0.1 reshape.41
  1.8 0.6 copy.11
  2.4 64.2 %shard_map.85 = (bf16[8,64,128]{2,1,0:T(8,128)(2,1)}, bf16[27,2,64,128]{3,2,1,0:T(8,128)(2,1)}, bf16[2,8,64,256]{3,2,1,0:T(8,128)(2,1)}) custom-call(bf16[8,64,128]{2,1,0:T(8,128)(2,1)} %bitcast.17, bf16[4,2,64,128]{3,2,1,0:T(8,128)(2,1)} %bitcast.18, bf16[9,384,128]{2,1,0:T(8,128)(2,1)} %bitcast.12, bf16[2,512,256]{2,1,0:T(8,128)(2,1)} %bitcast.14, ...), custom_call_target="tpu_custom_call" | custom-call | tf_op jit(solution)/shard_map/pallas_call | solution.py:527
  66.6 1.6 %copy.15 = bf16[1,8,64,128]{3,2,1,0:T(8,128)(2,1)} copy(bf16[1,8,64,128]{3,2,1,0:T(8,128)(2,1)} %bitcast.21) | data formatting | bytes 262144
  68.2 0.0 copy-start
  68.2 2.2 %copy.16 = bf16[3,3,3,128,128]{4,3,2,1,0:T(8,128)(2,1)} copy(bf16[3,3,3,128,128]{4,3,2,1,0:T(8,128)(2,1)} %bitcast.13) | data formatting | bytes 1769472
  70.4 0.0 copy-done
  70.4 0.8 %copy.17 = bf16[2,2,2,128,256]{4,3,2,1,0:T(8,128)(2,1)} copy(bf16[2,2,2,128,256]{4,3,2,1,0:T(8,128)(2,1)S(1)} %bitcast.15) | data formatting | bytes 1048576
Async XLA Ops:
  68.2 2.2 %copy-start = (bf16[2,8,64,256]{3,2,1,0:T(8,128)(2,1)S(1)}, bf16[2,8,64,256]{3,2,1,0:T(8,128)(2,1)}, u32[]{:S(2)}) copy-start(bf16[2,8,64,256]{3,2,1,0:T(8,128)(2,1)} %get-tuple-element.8) | copy-start | bytes 1572868

commit v3 on v2

--- a/solution.py
+++ b/solution.py
@@ -13,7 +13,9 @@
 ROWS = 64
 LANES = 128
 BLOCKS = 44
-PARTS = (("x", "y", "z", 0, 20), ("y", "x", "z", 20, 12), ("z", "x", "y", 32, 12))
+CONV = 28
+PARTS = (("x", "y", "z", 0, 16), ("y", "x", "z", 16, 12), ("z", "x", "y", 28, 16))
+PLANES = (1, 0, 2)
 
 
 def grid_sides(gz):
@@ -170,7 +172,7 @@
         conv_scale, down_scale = self.scales
         block = self.start + place.at["x"] * self.cut
         for i in range(self.cut):
-            scale = jnp.where(block + i < TAPS, jnp.float32(conv_scale), jnp.float32(down_scale))
+            scale = jnp.where(block + i < CONV, jnp.float32(conv_scale), jnp.float32(down_scale))
             mine[i] = (acc[i] / scale).astype(jnp.bfloat16)
         for step in place.steps(self.a2):
             to = place.ahead(self.a2, step)
@@ -206,19 +208,18 @@
             copy.wait_send()
 
 
-def store_results(result, conv_out, down_out, sems):
-    copies = []
+def store_kernel(rows_ref, result, input_out, conv_out, down_out, sems):
+    copies = [pltpu.make_async_copy(rows_ref, input_out, sems.at[0])]
     for core in range(2):
-        copies.append(
-            pltpu.make_async_copy(result.at[core, pl.ds(0, TAPS)], conv_out.at[:, core], sems.at[3 * core])
-        )
-        for half in range(2):
-            for_half = result.at[core, pl.ds(TAPS + 8 * half, 8)]
+        for place, kz in enumerate(PLANES):
+            source = result.at[core, pl.ds(9 * place, 9)]
             copies.append(
-                pltpu.make_async_copy(
-                    for_half, down_out.at[core, :, :, pl.ds(LANES * half, LANES)], sems.at[3 * core + 1 + half]
-                )
+                pltpu.make_async_copy(source, conv_out.at[pl.ds(9 * kz, 9), core], sems.at[len(copies)])
             )
+        for side in range(2):
+            source = result.at[core, pl.ds(CONV + 8 * side, 8)]
+            target = down_out.at[core, :, :, pl.ds(LANES * side, LANES)]
+            copies.append(pltpu.make_async_copy(source, target, sems.at[len(copies)]))
     for copy in copies:
         copy.start()
     for copy in copies:
@@ -290,15 +291,20 @@
     n,
     counts,
     scales,
-    level_ref,
+    level_hbm,
+    pre_hbm,
+    weight_hbm,
+    down_hbm,
+    skip_hbm,
+    deep_hbm,
+    input_rows,
+    result,
     pre_ref,
     weight_ref,
     down_ref,
     skip_ref,
     deep_ref,
-    input_out,
-    conv_out,
-    down_out,
+    deep_out,
     order,
     deep_in,
     deep_sorted,
@@ -307,23 +313,21 @@
     grad_pad,
     grad_wide,
     input_sum,
-    input_rows,
     conv_local,
     core_in,
     total,
-    result,
+    load_sems,
     deep_sems,
     plane_sems,
     level_sems,
     grad_sems,
     core_sems,
-    out_sems,
     *refs,
 ):
     place = Place(n)
     core = place.at["c"]
     partner = place.peer(c=1 - core)
-    rows, cols = level_ref.shape[0], level_ref.shape[1]
+    rows, cols = level_hbm.shape[0], level_hbm.shape[1]
     half = rows // 2 * cols
     level_halo = Halo(place, counts, level_pad, level_sems)
     grad_halo = Halo(place, counts, grad_pad, grad_sems)
@@ -345,8 +349,24 @@
             device = (place.gz + dz, place.at["x"] + dy)
             pl.semaphore_signal(barrier, inc=1, device_id=device, device_id_type=MESH)
 
+    level_ref = level_pad.at[1, pl.ds(1, rows)]
+    loads = []
+    for i, (source, target) in enumerate(
+        (
+            (deep_hbm, deep_ref),
+            (level_hbm, level_ref),
+            (down_hbm.at[core], down_ref),
+            (pre_hbm, pre_ref),
+            (skip_hbm, skip_ref),
+            (weight_hbm, weight_ref),
+        )
+    ):
+        loads.append(pltpu.make_async_copy(source, target, load_sems.at[i]))
+        loads[-1].start()
+
     wide = order.shape[0]
-    share_bits = (deep_ref.shape[1] // n["z"]).bit_length() - 1
+    share, deep_planes = deep_ref.shape[1], deep_ref.shape[2]
+    share_bits = share.bit_length() - 1
     y_bits, z_bits = n["y"].bit_length() - 1, n["z"].bit_length() - 1
     row = lax.broadcasted_iota(jnp.int32, (wide, wide), 0)
     col = lax.broadcasted_iota(jnp.int32, (wide, wide), 1)
@@ -357,10 +377,23 @@
     order[...] = jnp.where(col == wanted, 1.0, 0.0).astype(jnp.bfloat16)
     level_halo.clear()
     grad_halo.clear()
-    level_pad[1, pl.ds(1, rows)] = level_ref[...]
-    total[BLOCKS - 1] = jnp.zeros((ROWS, LANES), jnp.float32)
+    total[CONV - 1] = jnp.zeros((ROWS, LANES), jnp.float32)
     me_y, me_z = place.at["y"], place.at["z"]
-    deep_in[me_y, core] = deep_ref[me_y]
+
+    message = lax.broadcasted_iota(jnp.int32, (deep_planes * share, deep_planes), 0)
+    plane = lax.broadcasted_iota(jnp.int32, (deep_planes * share, deep_planes), 1)
+    plane_of = (bits(message, share_bits, z_bits) << y_bits) + bits(message, share_bits + z_bits, y_bits)
+    channel_of = bits(message, 0, share_bits)
+    loads[0].wait()
+    cells = deep_ref[...].astype(jnp.float32)
+    packed = None
+    for channel in range(share):
+        chosen = jnp.where((plane == plane_of) & (channel_of == channel), 1.0, 0.0).astype(jnp.bfloat16)
+        term = contract(chosen, cells[:, channel].astype(jnp.bfloat16), (1, 1))
+        packed = term if packed is None else packed + term
+    deep_out[...] = packed.astype(jnp.bfloat16).reshape(deep_out.shape)
+    deep_in[me_y, core] = deep_out[me_y]
+    loads[1].wait()
     pl.semaphore_wait(barrier, arrivals)
 
     sent = []
@@ -372,7 +405,7 @@
                 continue
             there = 1 - core if cross else core
             copy = remote(
-                deep_ref.at[to], deep_in.at[me_y, core], deep_sems, 2 * step + cross, place.peer(y=to, c=there)
+                deep_out.at[to], deep_in.at[me_y, core], deep_sems, 2 * step + cross, place.peer(y=to, c=there)
             )
             copy.start()
             sent.append(copy)
@@ -401,7 +434,26 @@
     covering = contract(spread, deep, (1, 1)).astype(jnp.bfloat16)
     column = lax.broadcasted_iota(jnp.int32, (half, LANES), 0) & (cols - 1)
     odd = (column & 1) == 1
-    down = contract(covering, down_ref[core], (1, 1))
+    loads[3].wait()
+    for b in range(2):
+        hidden = jnp.maximum(pre_ref[:, b].reshape(half, LANES).astype(jnp.float32), 0.0)
+        pair = jnp.concatenate([jnp.where(odd, 0.0, hidden), jnp.where(odd, hidden, 0.0)], axis=1)
+        slab = contract(pair.astype(jnp.bfloat16), covering, (0, 0))
+        for c in range(2):
+            for part in range(2):
+                for side in range(2):
+                    total[CONV + 8 * side + 2 * (2 * b + c) + part] = slab[
+                        c * LANES + part * ROWS : c * LANES + (part + 1) * ROWS, side * LANES : (side + 1) * LANES
+                    ]
+
+    parts = []
+    for i, part in enumerate(PARTS):
+        parts.append(PartSum(part, place, total, result.at[core], refs[i * PART_REFS : (i + 1) * PART_REFS], scales))
+    parts[2].scatter1()
+
+    loads[2].wait()
+    loads[4].wait()
+    down = contract(covering, down_ref[...], (1, 1))
     for b in range(2):
         even_part = down[:, 2 * b * LANES : (2 * b + 1) * LANES]
         odd_part = down[:, (2 * b + 1) * LANES : (2 * b + 2) * LANES]
@@ -419,7 +471,7 @@
 
     grads = grad_wide[...].reshape(rows * cols, 3 * LANES)
     swaps = [None] * 3
-    for kz in (1, 0, 2):
+    for kz in PLANES:
         if kz == 1:
             level_halo.receive(level_ref)
         for ky in range(3):
@@ -432,29 +484,16 @@
                     ]
         swaps[kz] = remote(conv_local.at[kz, 1 - core], core_in.at[kz], core_sems, kz, partner)
         swaps[kz].start()
-    for b in range(2):
-        hidden = jnp.maximum(pre_ref[:, b].reshape(half, LANES).astype(jnp.float32), 0.0)
-        pair = jnp.concatenate([jnp.where(odd, 0.0, hidden), jnp.where(odd, hidden, 0.0)], axis=1)
-        slab = contract(pair.astype(jnp.bfloat16), covering, (0, 0))
-        for c in range(2):
-            for part in range(2):
-                for side in range(2):
-                    total[TAPS + 8 * side + 2 * (2 * b + c) + part] = slab[
-                        c * LANES + part * ROWS : c * LANES + (part + 1) * ROWS, side * LANES : (side + 1) * LANES
-                    ]
-
-    parts = []
-    for i, part in enumerate(PARTS):
-        parts.append(PartSum(part, place, total, result.at[core], refs[i * PART_REFS : (i + 1) * PART_REFS], scales))
-    parts[2].scatter1()
-    for kz in (1, 0, 2):
+    for position, kz in enumerate(PLANES):
         swaps[kz].wait_recv()
         for tap in range(9):
-            total[9 * kz + tap] = conv_local[kz, core, tap] + core_in[kz, tap]
+            total[9 * position + tap] = conv_local[kz, core, tap] + core_in[kz, tap]
+        if position == 1:
+            parts[0].scatter1()
     parts[1].scatter1()
-    parts[0].scatter1()
 
     grad_halo.receive(own_rows)
+    loads[5].wait()
     for kz in range(3):
         acc = None
         for ky in range(3):
@@ -467,8 +506,6 @@
     _, behind = shifted(input_sum[:, 2 * LANES :], column, cols)
     sums = input_sum[:, LANES : 2 * LANES] + ahead + behind
     input_rows[...] = sums.astype(jnp.bfloat16).reshape(input_rows.shape)
-    input_copy = pltpu.make_async_copy(input_rows, input_out, out_sems.at[6])
-    input_copy.start()
 
     for stage in ("scatter2", "exchange3", "gather2"):
         for part in parts[::-1]:
@@ -483,8 +520,18 @@
         copy.wait_send()
     level_halo.finish(level_ref)
     grad_halo.finish(own_rows)
-    input_copy.wait()
-    store_results(result, conv_out, down_out, out_sems)
+
+
+def vmem_output(shape, dtype):
+    return pltpu.VMEM(shape, dtype)
+
+
+def in_vmem(array):
+    return pltpu.with_memory_space_constraint(array, pltpu.VMEM)
+
+
+def in_hbm(array):
+    return pltpu.with_memory_space_constraint(array, pltpu.HBM)
 
 
 def per_device(level_input, pre_activation, conv_weight, down_weight, skip_cotangent, deep_cotangent):
@@ -498,10 +545,14 @@
     scales = (math.sqrt(cell_total), math.sqrt(cell_total // 8))
     deep_cells = deep_rows * deep_cols
     wide = counts[0] * share
-    messages = deep_cotangent.reshape(side_z, side_y, deep_cells, share).transpose(1, 0, 3, 2)
-    messages = messages.reshape(side_y, side_z * share, deep_cells)
     pad = (3, rows + 2, cols, channels)
     scratch = [
+        pltpu.VMEM((rows // 2, 2, cols, channels), jnp.bfloat16),
+        pltpu.VMEM((9, 3 * channels, channels), jnp.bfloat16),
+        pltpu.VMEM((4 * channels, 2 * channels), jnp.bfloat16),
+        pltpu.VMEM((rows // 2, 2, cols, channels), jnp.bfloat16),
+        pltpu.VMEM((deep_cells, share, planes), jnp.bfloat16),
+        pltpu.VMEM((side_y, side_z * share, deep_cells), jnp.bfloat16),
         pltpu.VMEM((wide, wide), jnp.bfloat16),
         pltpu.VMEM((side_y, 2, side_z * share, deep_cells), jnp.bfloat16),
         pltpu.VMEM((side_z, side_y * 2 * share, deep_cells), jnp.bfloat16),
@@ -510,41 +561,49 @@
         pltpu.VMEM(pad, jnp.bfloat16),
         pltpu.VMEM((rows, cols, 3 * channels), jnp.bfloat16),
         pltpu.VMEM((cell_count, 3 * channels), jnp.float32),
-        pltpu.VMEM((rows, cols, channels), jnp.bfloat16),
         pltpu.VMEM((3, 2, 9, ROWS, LANES), jnp.float32),
         pltpu.VMEM((3, 9, ROWS, LANES), jnp.float32),
         pltpu.VMEM((BLOCKS, ROWS, LANES), jnp.float32),
-        pltpu.VMEM((2, BLOCKS, ROWS, LANES), jnp.bfloat16),
+        pltpu.SemaphoreType.DMA((6,)),
         pltpu.SemaphoreType.DMA((2, 2 * side_y)),
         pltpu.SemaphoreType.DMA((2, side_z)),
         pltpu.SemaphoreType.DMA((2, len(SIDES))),
         pltpu.SemaphoreType.DMA((2, len(SIDES))),
         pltpu.SemaphoreType.DMA((2, 3)),
-        pltpu.SemaphoreType.DMA((7,)),
     ]
     for part in PARTS:
         scratch += part_scratch(part, n)
+    input_rows, result = pl.pallas_call(
+        functools.partial(level_kernel, n, counts, scales),
+        out_shape=(
+            vmem_output((rows, cols, channels), jnp.bfloat16),
+            vmem_output((2, BLOCKS, ROWS, LANES), jnp.bfloat16),
+        ),
+        in_specs=[pl.BlockSpec(memory_space=pltpu.HBM)] * 6,
+        out_specs=[pl.BlockSpec(memory_space=pltpu.VMEM)] * 2,
+        scratch_shapes=scratch,
+        compiler_params=pltpu.CompilerParams(
+            collective_id=0, has_side_effects=True, vmem_limit_bytes=50 * 1024 * 1024
+        ),
+    )(
+        in_hbm(level_input.reshape(rows, cols, channels)),
+        in_hbm(pre_activation.reshape(rows // 2, 2, cols, channels)),
+        in_hbm(conv_weight.reshape(9, 3 * channels, channels)),
+        in_hbm(down_weight.reshape(2, 4 * channels, 2 * channels)),
+        in_hbm(skip_cotangent.reshape(rows // 2, 2, cols, channels)),
+        in_hbm(deep_cotangent.transpose(1, 2, 3, 0).reshape(deep_cells, share, planes)),
+    )
     input_grad, conv_grad, down_grad = pl.pallas_call(
-        functools.partial(level_kernel, n, counts, scales),
+        store_kernel,
         out_shape=(
             jax.ShapeDtypeStruct((rows, cols, channels), jnp.bfloat16),
             jax.ShapeDtypeStruct((TAPS, 2, ROWS, LANES), jnp.bfloat16),
             jax.ShapeDtypeStruct((2, 8, ROWS, 2 * LANES), jnp.bfloat16),
         ),
-        in_specs=[pl.BlockSpec(memory_space=pltpu.VMEM)] * 6,
+        in_specs=[pl.BlockSpec(memory_space=pltpu.VMEM)] * 2,
         out_specs=[pl.BlockSpec(memory_space=pl.ANY)] * 3,
-        scratch_shapes=scratch,
-        compiler_params=pltpu.CompilerParams(
-            collective_id=0, has_side_effects=True, vmem_limit_bytes=56 * 1024 * 1024
-        ),
-    )(
-        level_input.reshape(rows, cols, channels),
-        pre_activation.reshape(rows // 2, 2, cols, channels),
-        conv_weight.reshape(9, 3 * channels, channels),
-        down_weight.reshape(2, 4 * channels, 2 * channels),
-        skip_cotangent.reshape(rows // 2, 2, cols, channels),
-        messages,
-    )
+        scratch_shapes=[pltpu.SemaphoreType.DMA((11,))],
+    )(in_vmem(input_rows), in_vmem(result))
     return (
         input_grad.reshape(1, rows, cols, channels),
         conv_grad.reshape(3, 3, 3, channels, channels),

time: 71.5 us -> 62.1 us (0.87)
  local copies, waits for them, and re-layouts: 6.38 us -> 0 us
  Pallas kernels: 64.2 us -> 61.4 us
    unnamed x6 -> x0, local copies, waits for them, and re-layouts: 5.6 us -> none
    pallas_call x1, Pallas kernels: 64.2 us -> 60.1 us  [per_device(): pl.pallas_call(functools.partial(level_kernel, n, counts, scales), out_sh...]
    pallas_call x0 -> x1, Pallas kernels: none -> 1.22 us  [per_device(): pl.pallas_call(store_kernel, out_shape=(jax.ShapeDtypeStruct((rows, cols,...]
where the time goes in v3:
time: 62.1 us; the launch traced here: 62 us
  Pallas kernels  61.4 us (99%)
  between operations  0.64 us (1%)
    pallas_call x1, Pallas kernels, per_device(): pl.pallas_call(functools.partial(level_kernel, n, counts, scales), out_sh...  60.1 us

profile of v3, /device:TPU:1, one launch (start us, length us, event | category | flops | bytes accessed | tf_op | source)
XLA Modules:
  0.0 62.0 jit_solution(2088582456624972455)
XLA Ops:
  0.6 60.1 %shard_map.85 = (bf16[8,64,128]{2,1,0:T(8,128)(2,1)S(1)}, bf16[2,44,64,128]{3,2,1,0:T(8,128)(2,1)S(1)}) custom-call(bf16[8,64,128]{2,1,0:T(8,128)(2,1)} %bitcast.13, bf16[4,2,64,128]{3,2,1,0:T(8,128)(2,1)} %bitcast.14, bf16[9,384,128]{2,1,0:T(8,128)(2,1)} %bitcast.11, bf16[2,512,256]{2,1,0:T(8,128)(2,1)} %bitcast.12, bf16[4,2,64,128]{3,2,1,0:T(8,128)(2,1)} %bitcast.15, ...), custom_call_target="tpu_custom_call" | custom-call | tf_op jit(solution)/shard_map/pallas_call | solution.py:576
  60.8 1.2 %shard_map.86 = (bf16[8,64,128]{2,1,0:T(8,128)(2,1)}, bf16[27,2,64,128]{3,2,1,0:T(8,128)(2,1)}, bf16[2,8,64,256]{3,2,1,0:T(8,128)(2,1)}) custom-call(bf16[8,64,128]{2,1,0:T(8,128)(2,1)S(1)} %get-tuple-element.8.rows_ref, bf16[2,44,64,128]{3,2,1,0:T(8,128)(2,1)S(1)} %get-tuple-element.9.result), custom_call_target="tpu_custom_call" | custom-call | tf_op jit(solution)/shard_map/pallas_call | solution.py:596

commit v4 on v3

--- a/solution.py
+++ b/solution.py
@@ -14,7 +14,14 @@
 LANES = 128
 BLOCKS = 44
 CONV = 28
-PARTS = (("x", "y", "z", 0, 16), ("y", "x", "z", 16, 12), ("z", "x", "y", 28, 16))
+PARTS = (
+    ("x", "y", "z", 0, 8),
+    ("x", "z", "y", 8, 8),
+    ("y", "x", "z", 16, 12),
+    ("x", "z", "y", 28, 4),
+    ("z", "x", "y", 32, 12),
+)
+ORDER = (4, 3, 0, 1, 2)
 PLANES = (1, 0, 2)
 
 
@@ -78,7 +85,7 @@
         pltpu.VMEM((n[a1],) + first, jnp.bfloat16),
         pltpu.VMEM((n[a2],) + piece, jnp.float32),
         pltpu.VMEM((n[a2],) + piece, jnp.float32),
-        pltpu.VMEM((n[a3],) + piece, jnp.float32),
+        pltpu.VMEM((n[a3],) + piece, jnp.bfloat16),
         pltpu.SemaphoreType.DMA((2, n[a1])),
         pltpu.SemaphoreType.DMA((2, n[a2])),
         pltpu.SemaphoreType.DMA((2, n[a3])),
@@ -154,7 +161,8 @@
     def exchange3(self):
         place = self.place
         me = place.at[self.a3]
-        self.all3[me] = self.collect(self.in2, self.s2, self.a2, self.out2[place.at[self.a2]])
+        acc = self.collect(self.in2, self.s2, self.a2, self.out2[place.at[self.a2]])
+        self.all3[me] = acc.astype(jnp.bfloat16)
         for step in place.steps(self.a3):
             to = place.ahead(self.a3, step)
             self.start_copy(remote(self.all3.at[me], self.all3.at[me], self.s3, step, place.peer(**{self.a3: to})))
@@ -165,9 +173,9 @@
             source = place.behind(self.a3, step)
             ref = self.all3.at[source]
             remote(ref, ref, self.s3, step, place.peer(**{self.a3: source})).wait_recv()
-        acc = self.all3[0]
+        acc = self.all3[0].astype(jnp.float32)
         for source in range(1, place.n[self.a3]):
-            acc = acc + self.all3[source]
+            acc = acc + self.all3[source].astype(jnp.float32)
         mine = self.span(self.result, (self.a1, self.a2), place.at)
         conv_scale, down_scale = self.scales
         block = self.start + place.at["x"] * self.cut
@@ -178,7 +186,7 @@
             to = place.ahead(self.a2, step)
             self.start_copy(remote(mine, mine, self.g2, step, place.peer(**{self.a2: to})))
 
-    def gather1(self, partner_result):
+    def gather1(self):
         place = self.place
         for step in place.steps(self.a2)[::-1]:
             source = place.behind(self.a2, step)
@@ -312,6 +320,8 @@
     level_pad,
     grad_pad,
     grad_wide,
+    hidden_turned,
+    level_turned,
     input_sum,
     conv_local,
     core_in,
@@ -333,10 +343,12 @@
     grad_halo = Halo(place, counts, grad_pad, grad_sems)
 
     barrier = pltpu.get_barrier_semaphore()
-    peers = [partner]
-    for axis in "xyz":
+    peers = []
+    for step in place.steps("y"):
+        peers += [place.peer(y=place.ahead("y", step)), place.peer(y=place.ahead("y", step), c=1 - core)]
+    peers.append(partner)
+    for axis in "zx":
         peers += [place.peer(**{axis: place.ahead(axis, step)}) for step in place.steps(axis)]
-    peers += [place.peer(y=place.ahead("y", step), c=1 - core) for step in place.steps("y")]
     for device in peers:
         pl.semaphore_signal(barrier, inc=1, device_id=device, device_id_type=MESH)
     arrivals = len(peers)
@@ -423,6 +435,20 @@
         copy.start()
         sent.append(copy)
     deep_all[me_z] = deep_sorted[me_z]
+
+    column = lax.broadcasted_iota(jnp.int32, (half, LANES), 0) & (cols - 1)
+    odd = (column & 1) == 1
+    loads[3].wait()
+    for b in range(2):
+        hidden = jnp.maximum(pre_ref[:, b].reshape(half, LANES).astype(jnp.float32), 0.0)
+        for c in range(2):
+            chosen = jnp.where(odd, hidden, 0.0) if c else jnp.where(odd, 0.0, hidden)
+            hidden_turned[b, pl.ds(c * LANES, LANES)] = chosen.astype(jnp.bfloat16).T
+    level_halo.receive(level_ref)
+    for kz in PLANES:
+        for ky in range(3):
+            cells = level_pad[kz, pl.ds(ky, rows)].reshape(rows * cols, LANES)
+            level_turned[kz, pl.ds(ky * LANES, LANES)] = cells.T
     for step in place.steps("z")[::-1]:
         window = deep_all.at[place.behind("z", step)]
         remote(window, window, plane_sems, step, partner).wait_recv()
@@ -432,13 +458,8 @@
     spread = jnp.where(lax.shift_right_logical(cell, 1) == deep_cell, 1.0, 0.0).astype(jnp.bfloat16)
     deep = deep_all[...].reshape(wide, half // 2)
     covering = contract(spread, deep, (1, 1)).astype(jnp.bfloat16)
-    column = lax.broadcasted_iota(jnp.int32, (half, LANES), 0) & (cols - 1)
-    odd = (column & 1) == 1
-    loads[3].wait()
     for b in range(2):
-        hidden = jnp.maximum(pre_ref[:, b].reshape(half, LANES).astype(jnp.float32), 0.0)
-        pair = jnp.concatenate([jnp.where(odd, 0.0, hidden), jnp.where(odd, hidden, 0.0)], axis=1)
-        slab = contract(pair.astype(jnp.bfloat16), covering, (0, 0))
+        slab = contract(hidden_turned[b], covering, (1, 0))
         for c in range(2):
             for part in range(2):
                 for side in range(2):
@@ -449,7 +470,8 @@
     parts = []
     for i, part in enumerate(PARTS):
         parts.append(PartSum(part, place, total, result.at[core], refs[i * PART_REFS : (i + 1) * PART_REFS], scales))
-    parts[2].scatter1()
+    parts[4].scatter1()
+    parts[3].scatter1()
 
     loads[2].wait()
     loads[4].wait()
@@ -470,27 +492,29 @@
     grad_halo.send(own_rows)
 
     grads = grad_wide[...].reshape(rows * cols, 3 * LANES)
-    swaps = [None] * 3
-    for kz in PLANES:
-        if kz == 1:
-            level_halo.receive(level_ref)
+    swaps = []
+
+    def swapped(position):
+        swaps[position].wait_recv()
+        kz = PLANES[position]
+        for tap in range(9):
+            total[9 * position + tap] = conv_local[kz, core, tap] + core_in[kz, tap]
+
+    for position, kz in enumerate(PLANES):
+        slab = contract(level_turned[kz], grads, (1, 0))
         for ky in range(3):
-            cells = level_pad[kz, pl.ds(ky, rows)].reshape(rows * cols, LANES)
-            slab = contract(cells, grads, (0, 0))
             for kx in range(3):
                 for part in range(2):
                     conv_local[kz, part, 3 * ky + kx] = slab[
-                        part * ROWS : (part + 1) * ROWS, kx * LANES : (kx + 1) * LANES
+                        ky * LANES + part * ROWS : ky * LANES + (part + 1) * ROWS, kx * LANES : (kx + 1) * LANES
                     ]
-        swaps[kz] = remote(conv_local.at[kz, 1 - core], core_in.at[kz], core_sems, kz, partner)
-        swaps[kz].start()
-    for position, kz in enumerate(PLANES):
-        swaps[kz].wait_recv()
-        for tap in range(9):
-            total[9 * position + tap] = conv_local[kz, core, tap] + core_in[kz, tap]
-        if position == 1:
-            parts[0].scatter1()
-    parts[1].scatter1()
+        swaps.append(remote(conv_local.at[kz, 1 - core], core_in.at[kz], core_sems, kz, partner))
+        swaps[position].start()
+        if position:
+            swapped(position - 1)
+            parts[position - 1].scatter1()
+    swapped(2)
+    parts[2].scatter1()
 
     grad_halo.receive(own_rows)
     loads[5].wait()
@@ -507,14 +531,11 @@
     sums = input_sum[:, LANES : 2 * LANES] + ahead + behind
     input_rows[...] = sums.astype(jnp.bfloat16).reshape(input_rows.shape)
 
-    for stage in ("scatter2", "exchange3", "gather2"):
-        for part in parts[::-1]:
+    queue = [parts[i] for i in ORDER]
+    for stage in ("scatter2", "exchange3", "gather2", "gather1", "gather_core"):
+        for part in queue:
             getattr(part, stage)()
-    for part in parts[::-1]:
-        part.gather1(None)
-    for part in parts[::-1]:
-        part.gather_core()
-    for part in parts[::-1]:
+    for part in queue:
         part.finish(result.at[1 - core])
     for copy in sent + swaps:
         copy.wait_send()
@@ -560,6 +581,8 @@
         pltpu.VMEM(pad, jnp.bfloat16),
         pltpu.VMEM(pad, jnp.bfloat16),
         pltpu.VMEM((rows, cols, 3 * channels), jnp.bfloat16),
+        pltpu.VMEM((2, 2 * channels, cell_count // 2), jnp.bfloat16),
+        pltpu.VMEM((3, 3 * channels, cell_count), jnp.bfloat16),
         pltpu.VMEM((cell_count, 3 * channels), jnp.float32),
         pltpu.VMEM((3, 2, 9, ROWS, LANES), jnp.float32),
         pltpu.VMEM((3, 9, ROWS, LANES), jnp.float32),

time: 62.1 us -> 60.4 us (0.973)
  Pallas kernels: 61.4 us -> 59.7 us
    pallas_call x1, Pallas kernels: 60.1 us -> 58.4 us  [per_device(): pl.pallas_call(functools.partial(level_kernel, n, counts, scales), out_sh...]
where the time goes in v4:
time: 60.4 us; the launch traced here: 60.3 us
  Pallas kernels  59.7 us (99%)
  between operations  0.64 us (1%)
    pallas_call x1, Pallas kernels, per_device(): pl.pallas_call(functools.partial(level_kernel, n, counts, scales), out_sh...  58.4 us
    pallas_call x1, Pallas kernels, per_device(): pl.pallas_call(store_kernel, out_shape=(jax.ShapeDtypeStruct((rows, cols,...  1.22 us

profile of v4, /device:TPU:1, one launch (start us, length us, event | category | flops | bytes accessed | tf_op | source)
XLA Modules:
  0.0 60.3 jit_solution(6271800158635067818)
XLA Ops:
  0.6 58.4 %shard_map.85 = (bf16[8,64,128]{2,1,0:T(8,128)(2,1)S(1)}, bf16[2,44,64,128]{3,2,1,0:T(8,128)(2,1)S(1)}) custom-call(bf16[8,64,128]{2,1,0:T(8,128)(2,1)} %bitcast.13, bf16[4,2,64,128]{3,2,1,0:T(8,128)(2,1)} %bitcast.14, bf16[9,384,128]{2,1,0:T(8,128)(2,1)} %bitcast.11, bf16[2,512,256]{2,1,0:T(8,128)(2,1)} %bitcast.12, bf16[4,2,64,128]{3,2,1,0:T(8,128)(2,1)} %bitcast.15, ...), custom_call_target="tpu_custom_call" | custom-call | tf_op jit(solution)/shard_map/pallas_call | solution.py:599
  59.1 1.2 %shard_map.86 = (bf16[8,64,128]{2,1,0:T(8,128)(2,1)}, bf16[27,2,64,128]{3,2,1,0:T(8,128)(2,1)}, bf16[2,8,64,256]{3,2,1,0:T(8,128)(2,1)}) custom-call(bf16[8,64,128]{2,1,0:T(8,128)(2,1)S(1)} %get-tuple-element.8.rows_ref, bf16[2,44,64,128]{3,2,1,0:T(8,128)(2,1)S(1)} %get-tuple-element.9.result), custom_call_target="tpu_custom_call" | custom-call | tf_op jit(solution)/shard_map/pallas_call | solution.py:619

commit v5 on v4

--- a/solution.py
+++ b/solution.py
@@ -17,11 +17,12 @@
 PARTS = (
     ("x", "y", "z", 0, 8),
     ("x", "z", "y", 8, 8),
-    ("y", "x", "z", 16, 12),
+    ("x", "y", "z", 16, 4),
+    ("y", "x", "z", 20, 8),
     ("x", "z", "y", 28, 4),
     ("z", "x", "y", 32, 12),
 )
-ORDER = (4, 3, 0, 1, 2)
+ORDER = (5, 4, 0, 1, 2, 3)
 PLANES = (1, 0, 2)
 
 
@@ -57,15 +58,19 @@
         return sorted(range(1, count), key=lambda d: -min(d, count - d))
 
 
-def remote(src, dst, sems, slot, device):
+def remote(src, dst, send_sem, recv_sem, device):
     return pltpu.make_async_remote_copy(
         src_ref=src,
         dst_ref=dst,
-        send_sem=sems.at[0, slot],
-        recv_sem=sems.at[1, slot],
+        send_sem=send_sem,
+        recv_sem=recv_sem,
         device_id=device,
         device_id_type=MESH,
     )
+
+
+def wait_bytes(window, sem):
+    pltpu.make_async_copy(window, window, sem).wait()
 
 
 def part_shapes(part, n):
@@ -75,6 +80,13 @@
     piece = (cut, rows, LANES)
     first = (cut, ROWS, LANES) if a1 == "x" else (count, rows, LANES)
     return first, piece
+
+
+def part_rows(part, n):
+    a1, a2, a3, _, count = part
+    first, piece = (math.prod(shape) // LANES for shape in part_shapes(part, n))
+    stages = (n[a1] - 1) * first + (n[a2] - 1) * 2 * piece + (n[a3] - 1) * piece
+    return stages + (n[a2] - 1) * piece + (n[a1] - 1) * first + count * ROWS
 
 
 def part_scratch(part, n):
@@ -86,43 +98,37 @@
         pltpu.VMEM((n[a2],) + piece, jnp.float32),
         pltpu.VMEM((n[a2],) + piece, jnp.float32),
         pltpu.VMEM((n[a3],) + piece, jnp.bfloat16),
-        pltpu.SemaphoreType.DMA((2, n[a1])),
-        pltpu.SemaphoreType.DMA((2, n[a2])),
-        pltpu.SemaphoreType.DMA((2, n[a3])),
-        pltpu.SemaphoreType.DMA((2, n[a2])),
-        pltpu.SemaphoreType.DMA((2, n[a1])),
-        pltpu.SemaphoreType.DMA((2, n[a1])),
+        pltpu.SemaphoreType.DMA((7,)),
     ]
 
 
-PART_REFS = 11
+PART_REFS = 6
 
 
 class PartSum:
     def __init__(self, part, place, total, result, refs, scales):
         self.a1, self.a2, self.a3, self.start, self.count = part
+        self.part = part
         self.place = place
         self.total = total
         self.result = result
-        (self.out1, self.in1, self.out2, self.in2, self.all3) = refs[:5]
-        (self.s1, self.s2, self.s3, self.g2, self.g1, self.gc) = refs[5:]
+        self.out1, self.in1, self.out2, self.in2, self.all3, self.sems = refs
         self.rows = ROWS // place.n["y"]
         self.cut = self.count // place.n["x"]
         self.scales = scales
-        self.sent = []
-
-    def start_copy(self, copy):
-        copy.start()
-        self.sent.append(copy)
-
-    def span(self, ref, axes, where):
+
+    def send(self, src, dst, stage, **moved):
+        remote(src, dst, self.sems.at[6], self.sems.at[stage], self.place.peer(**moved)).start()
+
+    def span(self, ref, axes, where, times=1):
         blocks = pl.ds(self.start, self.count)
         rows = slice(None)
         for axis in axes:
+            wide = times if axis == axes[-1] else 1
             if axis == "x":
-                blocks = pl.ds(self.start + where["x"] * self.cut, self.cut)
+                blocks = pl.ds(self.start + where["x"] * self.cut, self.cut * wide)
             else:
-                rows = pl.ds(pl.multiple_of(where[axis] * self.rows, self.rows), self.rows)
+                rows = pl.ds(pl.multiple_of(where[axis] * self.rows, self.rows), self.rows * wide)
         return ref.at[blocks, rows]
 
     def scatter1(self):
@@ -130,23 +136,20 @@
         for step in place.steps(self.a1):
             to = place.ahead(self.a1, step)
             self.out1[to] = self.span(self.total, (self.a1,), {self.a1: to})[...].astype(jnp.bfloat16)
-            self.start_copy(
-                remote(self.out1.at[to], self.in1.at[place.at[self.a1]], self.s1, step, place.peer(**{self.a1: to}))
-            )
-
-    def collect(self, held, sems, axis, first):
+            self.send(self.out1.at[to], self.in1.at[place.at[self.a1]], 0, **{self.a1: to})
+
+    def collect(self, held, stage, axis, first):
         place = self.place
+        wait_bytes(held.at[pl.ds(0, place.n[axis] - 1)], self.sems.at[stage])
         acc = first
-        for step in place.steps(axis)[::-1]:
-            source = place.behind(axis, step)
-            remote(held.at[source], held.at[source], sems, step, place.peer(**{axis: source})).wait_recv()
-            acc = acc + held[source].astype(jnp.float32)
+        for step in place.steps(axis):
+            acc = acc + held[place.behind(axis, step)].astype(jnp.float32)
         return acc
 
     def scatter2(self):
         place = self.place
         own = self.span(self.total, (self.a1,), place.at)[...]
-        acc = self.collect(self.in1, self.s1, self.a1, own)
+        acc = self.collect(self.in1, 0, self.a1, own)
         for to in range(place.n[self.a2]):
             if self.a2 == "x":
                 self.out2[to] = acc[to * self.cut : (to + 1) * self.cut]
@@ -154,66 +157,48 @@
                 self.out2[to] = acc[:, to * self.rows : (to + 1) * self.rows]
         for step in place.steps(self.a2):
             to = place.ahead(self.a2, step)
-            self.start_copy(
-                remote(self.out2.at[to], self.in2.at[place.at[self.a2]], self.s2, step, place.peer(**{self.a2: to}))
-            )
+            self.send(self.out2.at[to], self.in2.at[place.at[self.a2]], 1, **{self.a2: to})
 
     def exchange3(self):
         place = self.place
         me = place.at[self.a3]
-        acc = self.collect(self.in2, self.s2, self.a2, self.out2[place.at[self.a2]])
+        acc = self.collect(self.in2, 1, self.a2, self.out2[place.at[self.a2]])
         self.all3[me] = acc.astype(jnp.bfloat16)
         for step in place.steps(self.a3):
-            to = place.ahead(self.a3, step)
-            self.start_copy(remote(self.all3.at[me], self.all3.at[me], self.s3, step, place.peer(**{self.a3: to})))
+            self.send(self.all3.at[me], self.all3.at[me], 2, **{self.a3: place.ahead(self.a3, step)})
 
     def gather2(self):
         place = self.place
-        for step in place.steps(self.a3)[::-1]:
-            source = place.behind(self.a3, step)
-            ref = self.all3.at[source]
-            remote(ref, ref, self.s3, step, place.peer(**{self.a3: source})).wait_recv()
+        wait_bytes(self.all3.at[pl.ds(0, place.n[self.a3] - 1)], self.sems.at[2])
         acc = self.all3[0].astype(jnp.float32)
         for source in range(1, place.n[self.a3]):
             acc = acc + self.all3[source].astype(jnp.float32)
         mine = self.span(self.result, (self.a1, self.a2), place.at)
         conv_scale, down_scale = self.scales
-        block = self.start + place.at["x"] * self.cut
-        for i in range(self.cut):
-            scale = jnp.where(block + i < CONV, jnp.float32(conv_scale), jnp.float32(down_scale))
-            mine[i] = (acc[i] / scale).astype(jnp.bfloat16)
+        scale = down_scale if self.start >= CONV else conv_scale
+        mine[...] = (acc / scale).astype(jnp.bfloat16)
         for step in place.steps(self.a2):
-            to = place.ahead(self.a2, step)
-            self.start_copy(remote(mine, mine, self.g2, step, place.peer(**{self.a2: to})))
+            self.send(mine, mine, 3, **{self.a2: place.ahead(self.a2, step)})
 
     def gather1(self):
         place = self.place
-        for step in place.steps(self.a2)[::-1]:
-            source = place.behind(self.a2, step)
-            ref = self.span(self.result, (self.a1, self.a2), dict(place.at, **{self.a2: source}))
-            remote(ref, ref, self.g2, step, place.peer(**{self.a2: source})).wait_recv()
+        zero = dict(place.at, **{self.a2: 0})
+        wait_bytes(self.span(self.result, (self.a1, self.a2), zero, place.n[self.a2] - 1), self.sems.at[3])
         mine = self.span(self.result, (self.a1,), place.at)
         for step in place.steps(self.a1):
-            to = place.ahead(self.a1, step)
-            self.start_copy(remote(mine, mine, self.g1, step, place.peer(**{self.a1: to})))
-        self.start_copy(remote(mine, mine, self.gc, 0, place.peer(c=1 - place.at["c"])))
+            self.send(mine, mine, 4, **{self.a1: place.ahead(self.a1, step)})
+        self.send(mine, mine, 5, c=1 - place.at["c"])
 
     def gather_core(self):
         place = self.place
-        for step in place.steps(self.a1)[::-1]:
-            source = place.behind(self.a1, step)
-            ref = self.span(self.result, (self.a1,), {self.a1: source})
-            remote(ref, ref, self.g1, step, place.peer(**{self.a1: source})).wait_recv()
-            self.start_copy(remote(ref, ref, self.gc, step, place.peer(c=1 - place.at["c"])))
-
-    def finish(self, other):
-        place = self.place
-        for step in [0] + place.steps(self.a1)[::-1]:
-            source = place.behind(self.a1, step)
-            ref = self.span(other, (self.a1,), {self.a1: source})
-            remote(ref, ref, self.gc, step, place.peer(c=1 - place.at["c"])).wait_recv()
-        for copy in self.sent:
-            copy.wait_send()
+        wait_bytes(self.span(self.result, (self.a1,), {self.a1: 0}, place.n[self.a1] - 1), self.sems.at[4])
+        for step in place.steps(self.a1):
+            ref = self.span(self.result, (self.a1,), {self.a1: place.behind(self.a1, step)})
+            self.send(ref, ref, 5, c=1 - place.at["c"])
+
+    def finish(self, other, dummy):
+        wait_bytes(other.at[pl.ds(self.start, self.count)], self.sems.at[5])
+        wait_bytes(dummy.at[pl.ds(0, part_rows(self.part, self.place.n))], self.sems.at[6])
 
 
 def store_kernel(rows_ref, result, input_out, conv_out, down_out, sems):
@@ -240,44 +225,43 @@
 class Halo:
     def __init__(self, place, counts, padded, sems):
         self.place, self.counts, self.padded, self.sems = place, counts, padded, sems
-
-    def has(self, dz, dy):
-        z, y = self.place.gz + dz, self.place.at["x"] + dy
-        return (z >= 0) & (z < self.counts[0]) & (y >= 0) & (y < self.counts[1])
-
-    def copy(self, i, rows):
-        dz, dy = SIDES[i]
-        depth = rows.shape[0]
-        if dy == 0:
-            src, dst = rows, self.padded.at[1 - dz, pl.ds(1, depth)]
-        elif dy == 1:
-            src, dst = rows.at[pl.ds(depth - 1, 1)], self.padded.at[1 - dz, pl.ds(0, 1)]
-        else:
-            src, dst = rows.at[pl.ds(0, 1)], self.padded.at[1 - dz, pl.ds(depth + 1, 1)]
-        device = (self.place.gz + dz, self.place.at["x"] + dy)
-        return remote(src, dst, self.sems, i, device)
-
-    def clear(self):
-        depth = self.padded.shape[1] - 2
-        for dz, dy in SIDES:
-            rows = {0: pl.ds(1, depth), 1: pl.ds(0, 1), -1: pl.ds(depth + 1, 1)}[dy]
-
-            @pl.when(jnp.logical_not(self.has(-dz, -dy)))
+        self.depth = padded.shape[1] - 2
+
+    def neighbour(self, dz, dy):
+        z, y = self.counts
+        return ((self.place.gz + dz + z) % z, (self.place.at["x"] + dy + y) % y)
+
+    def send(self, sides):
+        own = self.padded.at[1, pl.ds(1, self.depth)]
+        for dz, dy in sides:
+            if dy == 0:
+                src, dst = own, self.padded.at[1 - dz, pl.ds(1, self.depth)]
+            elif dy == 1:
+                src, dst = own.at[pl.ds(self.depth - 1, 1)], self.padded.at[1 - dz, pl.ds(0, 1)]
+            else:
+                src, dst = own.at[pl.ds(0, 1)], self.padded.at[1 - dz, pl.ds(self.depth + 1, 1)]
+            kind = 0 if dy == 0 else 1
+            remote(src, dst, self.sems.at[0, kind], self.sems.at[1, kind], self.neighbour(dz, dy)).start()
+
+    def wait(self, way):
+        wait_bytes(self.padded.at[pl.ds(0, 2), pl.ds(0, self.depth)], self.sems.at[way, 0])
+        wait_bytes(self.padded.at[pl.ds(0, 3), pl.ds(0, 2)], self.sems.at[way, 1])
+
+    def receive(self):
+        self.wait(1)
+        z, y = self.place.gz, self.place.at["x"]
+        everything = slice(None)
+        for edge, window in (
+            (z == 0, (0, everything)),
+            (z == self.counts[0] - 1, (2, everything)),
+            (y == 0, (everything, 0)),
+            (y == self.counts[1] - 1, (everything, self.depth + 1)),
+        ):
+
+            @pl.when(edge)
             def _():
-                window = self.padded.at[1 - dz, rows]
-                window[...] = jnp.zeros(window.shape, window.dtype)
-
-    def send(self, rows):
-        for i, side in enumerate(SIDES):
-            pl.when(self.has(*side))(self.copy(i, rows).start)
-
-    def receive(self, rows):
-        for i, (dz, dy) in enumerate(SIDES):
-            pl.when(self.has(-dz, -dy))(self.copy(i, rows).wait_recv)
-
-    def finish(self, rows):
-        for i, side in enumerate(SIDES):
-            pl.when(self.has(*side))(self.copy(i, rows).wait_send)
+                rows = self.padded.at[window]
+                rows[...] = jnp.zeros(rows.shape, rows.dtype)
 
 
 def contract(a, b, dims):
@@ -323,12 +307,13 @@
     hidden_turned,
     level_turned,
     input_sum,
-    conv_local,
+    conv_own,
+    conv_out,
     core_in,
     total,
+    dummy,
     load_sems,
     deep_sems,
-    plane_sems,
     level_sems,
     grad_sems,
     core_sems,
@@ -349,18 +334,9 @@
     peers.append(partner)
     for axis in "zx":
         peers += [place.peer(**{axis: place.ahead(axis, step)}) for step in place.steps(axis)]
+    peers += [level_halo.neighbour(dz, dy) for dz, dy in SIDES if dz]
     for device in peers:
         pl.semaphore_signal(barrier, inc=1, device_id=device, device_id_type=MESH)
-    arrivals = len(peers)
-    for dz, dy in SIDES:
-        near = level_halo.has(dz, dy)
-        arrivals = arrivals + near.astype(jnp.int32)
-
-        @pl.when(near)
-        def _():
-            device = (place.gz + dz, place.at["x"] + dy)
-            pl.semaphore_signal(barrier, inc=1, device_id=device, device_id_type=MESH)
-
     level_ref = level_pad.at[1, pl.ds(1, rows)]
     loads = []
     for i, (source, target) in enumerate(
@@ -380,16 +356,6 @@
     share, deep_planes = deep_ref.shape[1], deep_ref.shape[2]
     share_bits = share.bit_length() - 1
     y_bits, z_bits = n["y"].bit_length() - 1, n["z"].bit_length() - 1
-    row = lax.broadcasted_iota(jnp.int32, (wide, wide), 0)
-    col = lax.broadcasted_iota(jnp.int32, (wide, wide), 1)
-    low = bits(row, 0, share_bits)
-    source = bits(row, share_bits, 1 + y_bits)
-    target = bits(row, share_bits + 1 + y_bits, z_bits)
-    wanted = ((source << z_bits) + target << share_bits) + low
-    order[...] = jnp.where(col == wanted, 1.0, 0.0).astype(jnp.bfloat16)
-    level_halo.clear()
-    grad_halo.clear()
-    total[CONV - 1] = jnp.zeros((ROWS, LANES), jnp.float32)
     me_y, me_z = place.at["y"], place.at["z"]
 
     message = lax.broadcasted_iota(jnp.int32, (deep_planes * share, deep_planes), 0)
@@ -404,36 +370,32 @@
         term = contract(chosen, cells[:, channel].astype(jnp.bfloat16), (1, 1))
         packed = term if packed is None else packed + term
     deep_out[...] = packed.astype(jnp.bfloat16).reshape(deep_out.shape)
-    deep_in[me_y, core] = deep_out[me_y]
-    loads[1].wait()
-    pl.semaphore_wait(barrier, arrivals)
-
-    sent = []
-    first = []
+    deep_in[2 * me_y + core] = deep_out[me_y]
+    pl.semaphore_wait(barrier, len(peers))
+
     for step in place.steps("y") + [0]:
         to = place.ahead("y", step)
-        for cross in range(2):
-            if step == 0 and cross == 0:
-                continue
-            there = 1 - core if cross else core
-            copy = remote(
-                deep_out.at[to], deep_in.at[me_y, core], deep_sems, 2 * step + cross, place.peer(y=to, c=there)
-            )
-            copy.start()
-            sent.append(copy)
-            first.append((step, cross))
-    level_halo.send(level_ref)
-    for step, cross in first[::-1]:
-        origin = place.behind("y", step)
-        window = deep_in.at[origin, 1 - core if cross else core]
-        remote(window, window, deep_sems, 2 * step + cross, partner).wait_recv()
+        for there in (core, 1 - core) if step else (1 - core,):
+            remote(
+                deep_out.at[to], deep_in.at[2 * me_y + core], deep_sems.at[0], deep_sems.at[1], place.peer(y=to, c=there)
+            ).start()
+    row = lax.broadcasted_iota(jnp.int32, (wide, wide), 0)
+    col = lax.broadcasted_iota(jnp.int32, (wide, wide), 1)
+    low = bits(row, 0, share_bits)
+    source = bits(row, share_bits, 1 + y_bits)
+    target = bits(row, share_bits + 1 + y_bits, z_bits)
+    wanted = ((source << z_bits) + target << share_bits) + low
+    order[...] = jnp.where(col == wanted, 1.0, 0.0).astype(jnp.bfloat16)
+    total[CONV - 1] = jnp.zeros((ROWS, LANES), jnp.float32)
+    loads[1].wait()
+    messages = deep_in.at[pl.ds(0, 2 * n["y"] - 1)]
+    wait_bytes(messages, deep_sems.at[1])
     held = deep_in[...].reshape(wide, half // 2)
     deep_sorted[...] = contract(order[...], held, (1, 0)).astype(jnp.bfloat16).reshape(deep_sorted.shape)
     for step in place.steps("z"):
         to = place.ahead("z", step)
-        copy = remote(deep_sorted.at[to], deep_all.at[me_z], plane_sems, step, place.peer(z=to))
-        copy.start()
-        sent.append(copy)
+        remote(deep_sorted.at[to], deep_all.at[me_z], deep_sems.at[2], deep_sems.at[3], place.peer(z=to)).start()
+    level_halo.send(SIDES)
     deep_all[me_z] = deep_sorted[me_z]
 
     column = lax.broadcasted_iota(jnp.int32, (half, LANES), 0) & (cols - 1)
@@ -444,14 +406,13 @@
         for c in range(2):
             chosen = jnp.where(odd, hidden, 0.0) if c else jnp.where(odd, 0.0, hidden)
             hidden_turned[b, pl.ds(c * LANES, LANES)] = chosen.astype(jnp.bfloat16).T
-    level_halo.receive(level_ref)
+    level_halo.receive()
     for kz in PLANES:
         for ky in range(3):
             cells = level_pad[kz, pl.ds(ky, rows)].reshape(rows * cols, LANES)
             level_turned[kz, pl.ds(ky * LANES, LANES)] = cells.T
-    for step in place.steps("z")[::-1]:
-        window = deep_all.at[place.behind("z", step)]
-        remote(window, window, plane_sems, step, partner).wait_recv()
+    planes = deep_all.at[pl.ds(0, n["z"] - 1)]
+    wait_bytes(planes, deep_sems.at[3])
 
     cell = lax.broadcasted_iota(jnp.int32, (half, half // 2), 0)
     deep_cell = lax.broadcasted_iota(jnp.int32, (half, half // 2), 1)
@@ -470,8 +431,8 @@
     parts = []
     for i, part in enumerate(PARTS):
         parts.append(PartSum(part, place, total, result.at[core], refs[i * PART_REFS : (i + 1) * PART_REFS], scales))
+    parts[5].scatter1()
     parts[4].scatter1()
-    parts[3].scatter1()
 
     loads[2].wait()
     loads[4].wait()
@@ -488,35 +449,43 @@
             grad_wide[2 * y + b, :, 0:LANES] = ahead[span].astype(jnp.bfloat16)
             grad_wide[2 * y + b, :, LANES : 2 * LANES] = grad[span].astype(jnp.bfloat16)
             grad_wide[2 * y + b, :, 2 * LANES :] = behind[span].astype(jnp.bfloat16)
-    own_rows = grad_pad.at[1, pl.ds(1, rows)]
-    grad_halo.send(own_rows)
+    grad_halo.send([side for side in SIDES if side[1]])
+    near = [(1, 0), (-1, 0)]
+    for here in range(2):
+        pl.when(core == here)(functools.partial(grad_halo.send, [near[1 - here]]))
 
     grads = grad_wide[...].reshape(rows * cols, 3 * LANES)
     swaps = []
 
     def swapped(position):
+        kz = PLANES[position]
         swaps[position].wait_recv()
-        kz = PLANES[position]
         for tap in range(9):
-            total[9 * position + tap] = conv_local[kz, core, tap] + core_in[kz, tap]
+            total[9 * position + tap] = conv_own[kz, core, tap] + core_in[kz, tap].astype(jnp.float32)
 
     for position, kz in enumerate(PLANES):
         slab = contract(level_turned[kz], grads, (1, 0))
         for ky in range(3):
             for kx in range(3):
                 for part in range(2):
-                    conv_local[kz, part, 3 * ky + kx] = slab[
-                        ky * LANES + part * ROWS : ky * LANES + (part + 1) * ROWS, kx * LANES : (kx + 1) * LANES
-                    ]
-        swaps.append(remote(conv_local.at[kz, 1 - core], core_in.at[kz], core_sems, kz, partner))
+                    top = ky * LANES + part * ROWS
+                    block = slab[top : top + ROWS, kx * LANES : (kx + 1) * LANES]
+                    conv_own[kz, part, 3 * ky + kx] = block
+                    conv_out[kz, part, 3 * ky + kx] = block.astype(jnp.bfloat16)
+        swaps.append(
+            remote(conv_out.at[kz, 1 - core], core_in.at[kz], core_sems.at[0, kz], core_sems.at[1, kz], partner)
+        )
         swaps[position].start()
         if position:
             swapped(position - 1)
             parts[position - 1].scatter1()
+    for here in range(2):
+        pl.when(core == here)(functools.partial(grad_halo.send, [near[here]]))
     swapped(2)
     parts[2].scatter1()
-
-    grad_halo.receive(own_rows)
+    parts[3].scatter1()
+
+    grad_halo.receive()
     loads[5].wait()
     for kz in range(3):
         acc = None
@@ -536,11 +505,13 @@
         for part in queue:
             getattr(part, stage)()
     for part in queue:
-        part.finish(result.at[1 - core])
-    for copy in sent + swaps:
-        copy.wait_send()
-    level_halo.finish(level_ref)
-    grad_halo.finish(own_rows)
+        part.finish(result.at[1 - core], dummy)
+    for swap in swaps:
+        swap.wait_send()
+    wait_bytes(messages, deep_sems.at[0])
+    wait_bytes(planes, deep_sems.at[2])
+    level_halo.wait(0)
+    grad_halo.wait(0)
 
 
 def vmem_output(shape, dtype):
@@ -575,7 +546,7 @@
         pltpu.VMEM((deep_cells, share, planes), jnp.bfloat16),
         pltpu.VMEM((side_y, side_z * share, deep_cells), jnp.bfloat16),
         pltpu.VMEM((wide, wide), jnp.bfloat16),
-        pltpu.VMEM((side_y, 2, side_z * share, deep_cells), jnp.bfloat16),
+        pltpu.VMEM((2 * side_y, side_z * share, deep_cells), jnp.bfloat16),
         pltpu.VMEM((side_z, side_y * 2 * share, deep_cells), jnp.bfloat16),
         pltpu.VMEM((side_z, side_y * 2 * share, deep_cells), jnp.bfloat16),
         pltpu.VMEM(pad, jnp.bfloat16),
@@ -585,13 +556,14 @@
         pltpu.VMEM((3, 3 * channels, cell_count), jnp.bfloat16),
         pltpu.VMEM((cell_count, 3 * channels), jnp.float32),
         pltpu.VMEM((3, 2, 9, ROWS, LANES), jnp.float32),
-        pltpu.VMEM((3, 9, ROWS, LANES), jnp.float32),
+        pltpu.VMEM((3, 2, 9, ROWS, LANES), jnp.bfloat16),
+        pltpu.VMEM((3, 9, ROWS, LANES), jnp.bfloat16),
         pltpu.VMEM((BLOCKS, ROWS, LANES), jnp.float32),
+        pltpu.VMEM((max(part_rows(part, n) for part in PARTS), LANES), jnp.bfloat16),
         pltpu.SemaphoreType.DMA((6,)),
-        pltpu.SemaphoreType.DMA((2, 2 * side_y)),
-        pltpu.SemaphoreType.DMA((2, side_z)),
-        pltpu.SemaphoreType.DMA((2, len(SIDES))),
-        pltpu.SemaphoreType.DMA((2, len(SIDES))),
+        pltpu.SemaphoreType.DMA((4,)),
+        pltpu.SemaphoreType.DMA((2, 2)),
+        pltpu.SemaphoreType.DMA((2, 2)),
         pltpu.SemaphoreType.DMA((2, 3)),
     ]
     for part in PARTS:

time: 60.4 us -> 58.8 us (0.974)
  Pallas kernels: 59.7 us -> 58 us
    pallas_call x1, Pallas kernels: 58.4 us -> 56.8 us  [per_device(): pl.pallas_call(functools.partial(level_kernel, n, counts, scales), out_sh...]
where the time goes in v5:
time: 58.8 us; the launch traced here: 58.6 us
  Pallas kernels  58 us (99%)
  between operations  0.64 us (1%)
    pallas_call x1, Pallas kernels, per_device(): pl.pallas_call(functools.partial(level_kernel, n, counts, scales), out_sh...  56.8 us
    pallas_call x1, Pallas kernels, per_device(): pl.pallas_call(store_kernel, out_shape=(jax.ShapeDtypeStruct((rows, cols,...  1.22 us

profile of v5, /device:TPU:1, one launch (start us, length us, event | category | flops | bytes accessed | tf_op | source)
XLA Modules:
  0.0 58.6 jit_solution(4480014120693459789)
XLA Ops:
  0.6 56.8 %shard_map.85 = (bf16[8,64,128]{2,1,0:T(8,128)(2,1)S(1)}, bf16[2,44,64,128]{3,2,1,0:T(8,128)(2,1)S(1)}) custom-call(bf16[8,64,128]{2,1,0:T(8,128)(2,1)} %bitcast.13, bf16[4,2,64,128]{3,2,1,0:T(8,128)(2,1)} %bitcast.14, bf16[9,384,128]{2,1,0:T(8,128)(2,1)} %bitcast.11, bf16[2,512,256]{2,1,0:T(8,128)(2,1)} %bitcast.12, bf16[4,2,64,128]{3,2,1,0:T(8,128)(2,1)} %bitcast.15, ...), custom_call_target="tpu_custom_call" | custom-call | tf_op jit(solution)/shard_map/pallas_call | solution.py:571
  57.4 1.2 %shard_map.86 = (bf16[8,64,128]{2,1,0:T(8,128)(2,1)}, bf16[27,2,64,128]{3,2,1,0:T(8,128)(2,1)}, bf16[2,8,64,256]{3,2,1,0:T(8,128)(2,1)}) custom-call(bf16[8,64,128]{2,1,0:T(8,128)(2,1)S(1)} %get-tuple-element.8.rows_ref, bf16[2,44,64,128]{3,2,1,0:T(8,128)(2,1)S(1)} %get-tuple-element.9.result), custom_call_target="tpu_custom_call" | custom-call | tf_op jit(solution)/shard_map/pallas_call | solution.py:591

commit v6 on v5

--- a/solution.py
+++ b/solution.py
@@ -15,14 +15,14 @@
 BLOCKS = 44
 CONV = 28
 PARTS = (
-    ("x", "y", "z", 0, 8),
+    ("y", "x", "z", 0, 8),
     ("x", "z", "y", 8, 8),
-    ("x", "y", "z", 16, 4),
-    ("y", "x", "z", 20, 8),
+    ("x", "y", "z", 16, 12),
     ("x", "z", "y", 28, 4),
     ("z", "x", "y", 32, 12),
 )
-ORDER = (5, 4, 0, 1, 2, 3)
+FIRST = (3, 1, 4, 0, 2)
+LATER = (3, 4, 0, 1, 2)
 PLANES = (1, 0, 2)
 
 
@@ -85,7 +85,7 @@
 def part_rows(part, n):
     a1, a2, a3, _, count = part
     first, piece = (math.prod(shape) // LANES for shape in part_shapes(part, n))
-    stages = (n[a1] - 1) * first + (n[a2] - 1) * 2 * piece + (n[a3] - 1) * piece
+    stages = (n[a1] - 1) * first + (n[a2] - 1) * piece + (n[a3] - 1) * piece
     return stages + (n[a2] - 1) * piece + (n[a1] - 1) * first + count * ROWS
 
 
@@ -96,13 +96,14 @@
         pltpu.VMEM((n[a1],) + first, jnp.bfloat16),
         pltpu.VMEM((n[a1],) + first, jnp.bfloat16),
         pltpu.VMEM((n[a2],) + piece, jnp.float32),
-        pltpu.VMEM((n[a2],) + piece, jnp.float32),
+        pltpu.VMEM((n[a2],) + piece, jnp.bfloat16),
+        pltpu.VMEM((n[a2],) + piece, jnp.bfloat16),
         pltpu.VMEM((n[a3],) + piece, jnp.bfloat16),
         pltpu.SemaphoreType.DMA((7,)),
     ]
 
 
-PART_REFS = 6
+PART_REFS = 7
 
 
 class PartSum:
@@ -112,7 +113,7 @@
         self.place = place
         self.total = total
         self.result = result
-        self.out1, self.in1, self.out2, self.in2, self.all3, self.sems = refs
+        self.out1, self.in1, self.own2, self.out2, self.in2, self.all3, self.sems = refs
         self.rows = ROWS // place.n["y"]
         self.cut = self.count // place.n["x"]
         self.scales = scales
@@ -152,9 +153,11 @@
         acc = self.collect(self.in1, 0, self.a1, own)
         for to in range(place.n[self.a2]):
             if self.a2 == "x":
-                self.out2[to] = acc[to * self.cut : (to + 1) * self.cut]
+                piece = acc[to * self.cut : (to + 1) * self.cut]
             else:
-                self.out2[to] = acc[:, to * self.rows : (to + 1) * self.rows]
+                piece = acc[:, to * self.rows : (to + 1) * self.rows]
+            self.own2[to] = piece
+            self.out2[to] = piece.astype(jnp.bfloat16)
         for step in place.steps(self.a2):
             to = place.ahead(self.a2, step)
             self.send(self.out2.at[to], self.in2.at[place.at[self.a2]], 1, **{self.a2: to})
@@ -162,7 +165,7 @@
     def exchange3(self):
         place = self.place
         me = place.at[self.a3]
-        acc = self.collect(self.in2, 1, self.a2, self.out2[place.at[self.a2]])
+        acc = self.collect(self.in2, 1, self.a2, self.own2[place.at[self.a2]])
         self.all3[me] = acc.astype(jnp.bfloat16)
         for step in place.steps(self.a3):
             self.send(self.all3.at[me], self.all3.at[me], 2, **{self.a3: place.ahead(self.a3, step)})
@@ -327,16 +330,6 @@
     level_halo = Halo(place, counts, level_pad, level_sems)
     grad_halo = Halo(place, counts, grad_pad, grad_sems)
 
-    barrier = pltpu.get_barrier_semaphore()
-    peers = []
-    for step in place.steps("y"):
-        peers += [place.peer(y=place.ahead("y", step)), place.peer(y=place.ahead("y", step), c=1 - core)]
-    peers.append(partner)
-    for axis in "zx":
-        peers += [place.peer(**{axis: place.ahead(axis, step)}) for step in place.steps(axis)]
-    peers += [level_halo.neighbour(dz, dy) for dz, dy in SIDES if dz]
-    for device in peers:
-        pl.semaphore_signal(barrier, inc=1, device_id=device, device_id_type=MESH)
     level_ref = level_pad.at[1, pl.ds(1, rows)]
     loads = []
     for i, (source, target) in enumerate(
@@ -350,7 +343,20 @@
         )
     ):
         loads.append(pltpu.make_async_copy(source, target, load_sems.at[i]))
-        loads[-1].start()
+
+    loads[0].start()
+    barrier = pltpu.get_barrier_semaphore()
+    peers = []
+    for step in place.steps("y"):
+        peers += [place.peer(y=place.ahead("y", step)), place.peer(y=place.ahead("y", step), c=1 - core)]
+    peers.append(partner)
+    for axis in "zx":
+        peers += [place.peer(**{axis: place.ahead(axis, step)}) for step in place.steps(axis)]
+    peers += [level_halo.neighbour(dz, dy) for dz, dy in SIDES if dz]
+    for device in peers:
+        pl.semaphore_signal(barrier, inc=1, device_id=device, device_id_type=MESH)
+    for load in loads[1:]:
+        load.start()
 
     wide = order.shape[0]
     share, deep_planes = deep_ref.shape[1], deep_ref.shape[2]
@@ -379,6 +385,8 @@
             remote(
                 deep_out.at[to], deep_in.at[2 * me_y + core], deep_sems.at[0], deep_sems.at[1], place.peer(y=to, c=there)
             ).start()
+    loads[1].wait()
+    level_halo.send(SIDES)
     row = lax.broadcasted_iota(jnp.int32, (wide, wide), 0)
     col = lax.broadcasted_iota(jnp.int32, (wide, wide), 1)
     low = bits(row, 0, share_bits)
@@ -387,7 +395,6 @@
     wanted = ((source << z_bits) + target << share_bits) + low
     order[...] = jnp.where(col == wanted, 1.0, 0.0).astype(jnp.bfloat16)
     total[CONV - 1] = jnp.zeros((ROWS, LANES), jnp.float32)
-    loads[1].wait()
     messages = deep_in.at[pl.ds(0, 2 * n["y"] - 1)]
     wait_bytes(messages, deep_sems.at[1])
     held = deep_in[...].reshape(wide, half // 2)
@@ -395,7 +402,6 @@
     for step in place.steps("z"):
         to = place.ahead("z", step)
         remote(deep_sorted.at[to], deep_all.at[me_z], deep_sems.at[2], deep_sems.at[3], place.peer(z=to)).start()
-    level_halo.send(SIDES)
     deep_all[me_z] = deep_sorted[me_z]
 
     column = lax.broadcasted_iota(jnp.int32, (half, LANES), 0) & (cols - 1)
@@ -431,8 +437,8 @@
     parts = []
     for i, part in enumerate(PARTS):
         parts.append(PartSum(part, place, total, result.at[core], refs[i * PART_REFS : (i + 1) * PART_REFS], scales))
-    parts[5].scatter1()
     parts[4].scatter1()
+    parts[3].scatter1()
 
     loads[2].wait()
     loads[4].wait()
@@ -483,7 +489,9 @@
         pl.when(core == here)(functools.partial(grad_halo.send, [near[here]]))
     swapped(2)
     parts[2].scatter1()
-    parts[3].scatter1()
+
+    for i in FIRST:
+        parts[i].scatter2()
 
     grad_halo.receive()
     loads[5].wait()
@@ -500,8 +508,8 @@
     sums = input_sum[:, LANES : 2 * LANES] + ahead + behind
     input_rows[...] = sums.astype(jnp.bfloat16).reshape(input_rows.shape)
 
-    queue = [parts[i] for i in ORDER]
-    for stage in ("scatter2", "exchange3", "gather2", "gather1", "gather_core"):
+    queue = [parts[i] for i in LATER]
+    for stage in ("exchange3", "gather2", "gather1", "gather_core"):
         for part in queue:
             getattr(part, stage)()
     for part in queue:

time: 58.8 us -> 56 us (0.952)
  Pallas kernels: 58 us -> 55.2 us
    pallas_call x1, Pallas kernels: 56.8 us -> 54 us  [per_device(): pl.pallas_call(functools.partial(level_kernel, n, counts, scales), out_sh...]
where the time goes in v6:
time: 56 us; the launch traced here: 55.9 us
  Pallas kernels  55.2 us (99%)
  between operations  0.64 us (1%)
    pallas_call x1, Pallas kernels, per_device(): pl.pallas_call(functools.partial(level_kernel, n, counts, scales), out_sh...  54 us
    pallas_call x1, Pallas kernels, per_device(): pl.pallas_call(store_kernel, out_shape=(jax.ShapeDtypeStruct((rows, cols,...  1.22 us

profile of v6, /device:TPU:1, one launch (start us, length us, event | category | flops | bytes accessed | tf_op | source)
XLA Modules:
  0.0 55.9 jit_solution(9340276865727823451)
XLA Ops:
  0.6 54.0 %shard_map.85 = (bf16[8,64,128]{2,1,0:T(8,128)(2,1)S(1)}, bf16[2,44,64,128]{3,2,1,0:T(8,128)(2,1)S(1)}) custom-call(bf16[8,64,128]{2,1,0:T(8,128)(2,1)} %bitcast.13, bf16[4,2,64,128]{3,2,1,0:T(8,128)(2,1)} %bitcast.14, bf16[9,384,128]{2,1,0:T(8,128)(2,1)} %bitcast.11, bf16[2,512,256]{2,1,0:T(8,128)(2,1)} %bitcast.12, bf16[4,2,64,128]{3,2,1,0:T(8,128)(2,1)} %bitcast.15, ...), custom_call_target="tpu_custom_call" | custom-call | tf_op jit(solution)/shard_map/pallas_call | solution.py:579
  54.6 1.2 %shard_map.86 = (bf16[8,64,128]{2,1,0:T(8,128)(2,1)}, bf16[27,2,64,128]{3,2,1,0:T(8,128)(2,1)}, bf16[2,8,64,256]{3,2,1,0:T(8,128)(2,1)}) custom-call(bf16[8,64,128]{2,1,0:T(8,128)(2,1)S(1)} %get-tuple-element.8.rows_ref, bf16[2,44,64,128]{3,2,1,0:T(8,128)(2,1)S(1)} %get-tuple-element.9.result), custom_call_target="tpu_custom_call" | custom-call | tf_op jit(solution)/shard_map/pallas_call | solution.py:599

commit v7 on v6

--- a/solution.py
+++ b/solution.py
@@ -21,8 +21,12 @@
     ("x", "z", "y", 28, 4),
     ("z", "x", "y", 32, 12),
 )
-FIRST = (3, 1, 4, 0, 2)
-LATER = (3, 4, 0, 1, 2)
+STAGES = (
+    ("exchange3", (3, 0, 1, 4, 2)),
+    ("gather2", (3, 0, 1, 4, 2)),
+    ("gather1", (3, 0, 4, 1, 2)),
+    ("gather_core", (3, 0, 1, 4, 2)),
+)
 PLANES = (1, 0, 2)
 
 
@@ -482,15 +486,13 @@
             remote(conv_out.at[kz, 1 - core], core_in.at[kz], core_sems.at[0, kz], core_sems.at[1, kz], partner)
         )
         swaps[position].start()
-        if position:
-            swapped(position - 1)
-            parts[position - 1].scatter1()
+    for position in range(3):
+        swapped(position)
+        parts[position].scatter1()
     for here in range(2):
         pl.when(core == here)(functools.partial(grad_halo.send, [near[here]]))
-    swapped(2)
-    parts[2].scatter1()
-
-    for i in FIRST:
+
+    for i in (3, 1, 0, 2, 4):
         parts[i].scatter2()
 
     grad_halo.receive()
@@ -508,11 +510,10 @@
     sums = input_sum[:, LANES : 2 * LANES] + ahead + behind
     input_rows[...] = sums.astype(jnp.bfloat16).reshape(input_rows.shape)
 
-    queue = [parts[i] for i in LATER]
-    for stage in ("exchange3", "gather2", "gather1", "gather_core"):
-        for part in queue:
-            getattr(part, stage)()
-    for part in queue:
+    for stage, queue in STAGES:
+        for i in queue:
+            getattr(parts[i], stage)()
+    for part in parts:
         part.finish(result.at[1 - core], dummy)
     for swap in swaps:
         swap.wait_send()

time: 56 us -> 56 us (level)
  no operation moved by 1% of the time
where the time goes in v7:
time: 56 us; the launch traced here: 55.9 us
  Pallas kernels  55.2 us (99%)
  between operations  0.64 us (1%)
    pallas_call x1, Pallas kernels, per_device(): pl.pallas_call(functools.partial(level_kernel, n, counts, scales), out_sh...  54 us
    pallas_call x1, Pallas kernels, per_device(): pl.pallas_call(store_kernel, out_shape=(jax.ShapeDtypeStruct((rows, cols,...  1.22 us

profile of v7, /device:TPU:1, one launch (start us, length us, event | category | flops | bytes accessed | tf_op | source)
XLA Modules:
  0.0 55.9 jit_solution(13379283900594888335)
XLA Ops:
  0.6 54.0 %shard_map.85 = (bf16[8,64,128]{2,1,0:T(8,128)(2,1)S(1)}, bf16[2,44,64,128]{3,2,1,0:T(8,128)(2,1)S(1)}) custom-call(bf16[8,64,128]{2,1,0:T(8,128)(2,1)} %bitcast.13, bf16[4,2,64,128]{3,2,1,0:T(8,128)(2,1)} %bitcast.14, bf16[9,384,128]{2,1,0:T(8,128)(2,1)} %bitcast.11, bf16[2,512,256]{2,1,0:T(8,128)(2,1)} %bitcast.12, bf16[4,2,64,128]{3,2,1,0:T(8,128)(2,1)} %bitcast.15, ...), custom_call_target="tpu_custom_call" | custom-call | tf_op jit(solution)/shard_map/pallas_call | solution.py:580
  54.7 1.2 %shard_map.86 = (bf16[8,64,128]{2,1,0:T(8,128)(2,1)}, bf16[27,2,64,128]{3,2,1,0:T(8,128)(2,1)}, bf16[2,8,64,256]{3,2,1,0:T(8,128)(2,1)}) custom-call(bf16[8,64,128]{2,1,0:T(8,128)(2,1)S(1)} %get-tuple-element.8.rows_ref, bf16[2,44,64,128]{3,2,1,0:T(8,128)(2,1)S(1)} %get-tuple-element.9.result), custom_call_target="tpu_custom_call" | custom-call | tf_op jit(solution)/shard_map/pallas_call | solution.py:600
